TPU v7x, 32 devices: a whole 2x2x4 slice. The times are simulated.
32 devices in a mesh: ctx: 8 (over y, x, core), fsdp: 4 (over z).
Axes of the slice: x: 2, y: 2, z: 4, core: 2. Of those that a mesh axis runs over, the one named last changes fastest.
Arguments:
- layer_in: bfloat16 [4, 1024, 1600], P('fsdp', 'ctx'), may hold values from -6 to 6
- out_cot: bfloat16 [4, 1024, 1600], P('fsdp', 'ctx'), may hold values from -6 to 6
- first_gain: bfloat16 [1600], P('fsdp'), may hold values from 0.5 to 1.5
- first_bias: bfloat16 [1600], P('fsdp'), may hold values from -3 to 3
- qkv_weight: bfloat16 [1600, 4800], P('fsdp'), may hold values from -0.15625 to 0.15625
- qv_bias: bfloat16 [2, 1600], P(None, 'fsdp'), may hold values from -3 to 3
- out_weight: bfloat16 [1600, 1600], P('fsdp'), may hold values from -0.625 to 0.625
- out_bias: bfloat16 [1600], P('fsdp'), may hold values from -3 to 3
- second_gain: bfloat16 [1600], P('fsdp'), may hold values from 0.5 to 1.5
- second_bias: bfloat16 [1600], P('fsdp'), may hold values from -3 to 3
- fc_weight: bfloat16 [1600, 6400], P('fsdp'), may hold values from -0.15625 to 0.15625
- fc_bias: bfloat16 [6400], P('fsdp'), may hold values from -3 to 3
- proj_weight: bfloat16 [6400, 1600], P(None, 'fsdp'), may hold values from -0.078125 to 0.078125
- proj_bias: bfloat16 [1600], P('fsdp'), may hold values from -3 to 3
Outputs:
- layer_out: bfloat16 [4, 1024, 1600], P('fsdp', 'ctx')
- grad_in: bfloat16 [4, 1024, 1600], P('fsdp', 'ctx')
- grad_first_gain: float32 [1600], P('fsdp')
- grad_first_bias: float32 [1600], P('fsdp')
- grad_qkv_weight: float32 [1600, 4800], P('fsdp')
- grad_qv_bias: float32 [2, 1600], P(None, 'fsdp')
- grad_out_weight: float32 [1600, 1600], P('fsdp')
- grad_out_bias: float32 [1600], P('fsdp')
- grad_second_gain: float32 [1600], P('fsdp')
- grad_second_bias: float32 [1600], P('fsdp')
- grad_fc_weight: float32 [1600, 6400], P('fsdp')
- grad_fc_bias: float32 [6400], P('fsdp')
- grad_proj_weight: float32 [6400, 1600], P(None, 'fsdp')
- grad_proj_bias: float32 [1600], P('fsdp')
All inputs are finite; a program needn't handle non-finite values.
Results may differ from a plain program's by a relative error of at most 0.03.
Values may be sent and summed in bfloat16 or wider, within the bound.
No kernel may reach another device: no remote copies, remote signals or barrier semaphores. Data moves between devices by JAX's collectives and lax.ppermute only.
A program may use at most 512 MiB of HBM per device.

v0:
```python
import math

import jax
import jax.numpy as jnp
from jax import lax
from jax.sharding import PartitionSpec as P

D = 1600
H = 25
HD = 64


def norm_apply(values, norm_gain, norm_bias):
    centre = jnp.mean(values, axis=-1, keepdims=True)
    shifted = values - centre
    spread = jnp.mean(shifted * shifted, axis=-1, keepdims=True)
    return shifted * lax.rsqrt(spread + 1e-05) * norm_gain + norm_bias


def contract_rows(left, right):
    return lax.dot_general(
        left, right, (((0,), (0,)), ((), ())), preferred_element_type=jnp.float32
    )


def contract_cols(left, right):
    return lax.dot_general(
        left, right, (((1,), (1,)), ((), ())), preferred_element_type=jnp.float32
    )


def split_product(form, weights, other):
    upper = weights.astype(jnp.bfloat16)
    lower = (weights - upper.astype(jnp.float32)).astype(jnp.bfloat16)
    return jnp.einsum(form, upper, other, preferred_element_type=jnp.float32) + jnp.einsum(
        form, lower, other, preferred_element_type=jnp.float32
    )


def sweep_blocks(running, piece_rows, handle):
    block_rows = 512
    return lax.fori_loop(
        0,
        piece_rows // block_rows,
        lambda block_index, state_now: handle(state_now, block_index * block_rows, block_rows),
        running,
    )


def on_device(
    layer_in,
    out_cot,
    first_gain,
    first_bias,
    qkv_weight,
    qv_bias,
    out_weight,
    out_bias,
    second_gain,
    second_bias,
    fc_weight,
    fc_bias,
    proj_weight,
    proj_bias,
):
    f32 = jnp.float32
    bf16 = jnp.bfloat16
    factor = 1.0 / math.sqrt(HD)
    gathered = (
        lax.all_gather(first_gain, "fsdp", axis=0, tiled=True),
        lax.all_gather(first_bias, "fsdp", axis=0, tiled=True),
        lax.all_gather(qkv_weight, "fsdp", axis=0, tiled=True),
        lax.all_gather(qv_bias, "fsdp", axis=1, tiled=True),
        lax.all_gather(out_weight, "fsdp", axis=0, tiled=True),
        lax.all_gather(out_bias, "fsdp", axis=0, tiled=True),
        lax.all_gather(second_gain, "fsdp", axis=0, tiled=True),
        lax.all_gather(second_bias, "fsdp", axis=0, tiled=True),
        lax.all_gather(fc_weight, "fsdp", axis=0, tiled=True),
        lax.all_gather(fc_bias, "fsdp", axis=0, tiled=True),
        lax.all_gather(proj_weight, "fsdp", axis=1, tiled=True),
        lax.all_gather(proj_bias, "fsdp", axis=0, tiled=True),
    )
    gain_one = gathered[0].astype(f32)
    bias_one = gathered[1].astype(f32)
    full_qkv = gathered[2]
    bias_qv = gathered[3].astype(f32)
    full_out = gathered[4]
    bias_out = gathered[5].astype(f32)
    gain_two = gathered[6].astype(f32)
    bias_two = gathered[7].astype(f32)
    full_fc = gathered[8]
    bias_fc = gathered[9].astype(f32)
    full_proj = gathered[10]
    bias_proj = gathered[11].astype(f32)
    tokens = layer_in[0].astype(f32)
    local_rows = tokens.shape[0]
    offset = lax.axis_index("ctx") * local_rows
    query_pos = offset + jnp.arange(local_rows, dtype=jnp.int32)
    normed_one = norm_apply(tokens, gain_one, bias_one).astype(bf16)
    projected = jnp.dot(normed_one, full_qkv, preferred_element_type=f32)
    queries = (projected[:, 0:D] + bias_qv[0]).astype(bf16)
    key_rows = projected[:, D : 2 * D].astype(bf16)
    value_rows = (projected[:, 2 * D : 3 * D] + bias_qv[1]).astype(bf16)
    query_heads = queries.reshape(local_rows, H, HD)
    start_state = (
        jnp.full((H, local_rows), -1e30, f32),
        jnp.zeros((H, local_rows), f32),
        jnp.zeros((local_rows, H, HD), f32),
    )
    key_piece = lax.all_gather(key_rows, "ctx", axis=0, tiled=True)
    value_piece = lax.all_gather(value_rows, "ctx", axis=0, tiled=True)

    def forward_step(state_now, begin_row, block_rows):
        row_max, row_total, accum = state_now
        key_block = lax.dynamic_slice_in_dim(key_piece, begin_row, block_rows, 0).reshape(
            block_rows, H, HD
        )
        value_block = lax.dynamic_slice_in_dim(value_piece, begin_row, block_rows, 0).reshape(
            block_rows, H, HD
        )
        key_pos = begin_row + jnp.arange(block_rows, dtype=jnp.int32)
        allowed = (key_pos[None, :] <= query_pos[:, None])[None]
        scores = (
            jnp.einsum("qhd,khd->hqk", query_heads, key_block, preferred_element_type=f32) * factor
        )
        masked = jnp.where(allowed, scores, -1e30)
        new_max = jnp.maximum(row_max, jnp.max(masked, axis=-1))
        weights = jnp.where(allowed, jnp.exp(masked - new_max[:, :, None]), 0.0)
        rescale = jnp.exp(row_max - new_max)
        new_total = row_total * rescale + jnp.sum(weights, axis=-1)
        update = split_product("hqk,khd->qhd", weights, value_block)
        new_accum = accum * rescale.T[:, :, None] + update
        return (new_max, new_total, new_accum)

    row_max, row_total, accum = sweep_blocks(start_state, key_piece.shape[0], forward_step)
    attn_heads = accum / row_total.T[:, :, None]
    log_total = row_max + jnp.log(row_total)
    attn_out = attn_heads.reshape(local_rows, D).astype(bf16)
    resid = tokens + jnp.dot(attn_out, full_out, preferred_element_type=f32) + bias_out
    normed_two = norm_apply(resid, gain_two, bias_two).astype(bf16)
    pre_act = jnp.dot(normed_two, full_fc, preferred_element_type=f32) + bias_fc
    activated = jax.nn.gelu(pre_act, approximate=True).astype(bf16)
    mlp_out = jnp.dot(activated, full_proj, preferred_element_type=f32) + bias_proj
    layer_out = (resid + mlp_out).astype(bf16)[None]
    cotangent = out_cot[0]
    cot_float = cotangent.astype(f32)
    grad_proj = contract_rows(activated, cotangent)
    grad_proj_b = jnp.sum(cot_float, axis=0)
    d_activated = contract_cols(cotangent, full_proj)
    unused_value, gelu_back = jax.vjp(lambda inner: jax.nn.gelu(inner, approximate=True), pre_act)
    d_pre = gelu_back(d_activated)[0].astype(bf16)
    grad_fc = contract_rows(normed_two, d_pre)
    grad_fc_b = jnp.sum(d_pre.astype(f32), axis=0)
    d_norm_two = contract_cols(d_pre, full_fc)
    unused_two, norm_back_two = jax.vjp(norm_apply, resid, gain_two, bias_two)
    d_resid_norm, grad_gain_two, grad_bias_two = norm_back_two(d_norm_two)
    d_resid = cot_float + d_resid_norm
    d_branch = d_resid.astype(bf16)
    mlp_parts = (
        lax.psum_scatter(
            grad_gain_two.astype(jnp.bfloat16), "fsdp", scatter_dimension=0, tiled=True
        ).astype(jnp.float32),
        lax.psum_scatter(
            grad_bias_two.astype(jnp.bfloat16), "fsdp", scatter_dimension=0, tiled=True
        ).astype(jnp.float32),
        lax.psum_scatter(
            grad_fc.astype(jnp.bfloat16), "fsdp", scatter_dimension=0, tiled=True
        ).astype(jnp.float32),
        lax.psum_scatter(
            grad_fc_b.astype(jnp.bfloat16), "fsdp", scatter_dimension=0, tiled=True
        ).astype(jnp.float32),
        lax.psum_scatter(
            grad_proj.astype(jnp.bfloat16), "fsdp", scatter_dimension=1, tiled=True
        ).astype(jnp.float32),
        lax.psum_scatter(
            grad_proj_b.astype(jnp.bfloat16), "fsdp", scatter_dimension=0, tiled=True
        ).astype(jnp.float32),
    )
    mlp_parts = (
        lax.psum(mlp_parts[0].astype(jnp.bfloat16), "ctx").astype(jnp.float32),
        lax.psum(mlp_parts[1].astype(jnp.bfloat16), "ctx").astype(jnp.float32),
        lax.psum(mlp_parts[2].astype(jnp.bfloat16), "ctx").astype(jnp.float32),
        lax.psum(mlp_parts[3].astype(jnp.bfloat16), "ctx").astype(jnp.float32),
        lax.psum(mlp_parts[4].astype(jnp.bfloat16), "ctx").astype(jnp.float32),
        lax.psum(mlp_parts[5].astype(jnp.bfloat16), "ctx").astype(jnp.float32),
    )
    grad_out = contract_rows(attn_out, d_branch)
    grad_out_b = jnp.sum(d_branch.astype(f32), axis=0)
    d_attn = contract_cols(d_branch, full_out).astype(bf16)
    d_attn_heads = d_attn.reshape(local_rows, H, HD)
    delta_cols = jnp.sum(d_attn_heads.astype(f32) * attn_heads, axis=-1)
    delta_rows = delta_cols.T
    seq_rows = lax.axis_size("ctx") * local_rows

    def block_weights(query_block, key_block, lse_block, query_at, key_at):
        allowed = (key_at[None, :] <= query_at[:, None])[None]
        scores = (
            jnp.einsum("qhd,khd->hqk", query_block, key_block, preferred_element_type=f32) * factor
        )
        return jnp.where(allowed, jnp.exp(scores - lse_block[:, :, None]), 0.0)

    buffer_start = jnp.zeros((seq_rows, 2 * D), f32)
    back_start = (jnp.zeros((local_rows, H, HD), f32), buffer_start)
    query_key_piece = lax.all_gather(key_rows, "ctx", axis=0, tiled=True)
    query_value_piece = lax.all_gather(value_rows, "ctx", axis=0, tiled=True)

    def backward_step(state_now, begin_row, block_rows):
        d_query_sum, kv_buffer = state_now
        key_block = lax.dynamic_slice_in_dim(query_key_piece, begin_row, block_rows, 0).reshape(
            block_rows, H, HD
        )
        value_block = lax.dynamic_slice_in_dim(query_value_piece, begin_row, block_rows, 0).reshape(
            block_rows, H, HD
        )
        key_pos = begin_row + jnp.arange(block_rows, dtype=jnp.int32)
        weights = block_weights(query_heads, key_block, log_total, query_pos, key_pos)
        d_weights = jnp.einsum(
            "qhd,khd->hqk", d_attn_heads, value_block, preferred_element_type=f32
        )
        d_scores = (weights * (d_weights - delta_rows[:, :, None])).astype(bf16)
        d_query_sum = (
            d_query_sum
            + jnp.einsum("hqk,khd->qhd", d_scores, key_block, preferred_element_type=f32) * factor
        )
        d_key_block = (
            jnp.einsum("hqk,qhd->khd", d_scores, query_heads, preferred_element_type=f32) * factor
        )
        d_value_block = split_product("hqk,qhd->khd", weights, d_attn_heads)
        zero_col = jnp.zeros((), jnp.int32)
        current = lax.dynamic_slice(kv_buffer, (begin_row, zero_col), (block_rows, 2 * D))
        added = current + jnp.concatenate(
            [d_key_block.reshape(block_rows, D), d_value_block.reshape(block_rows, D)], axis=1
        )
        kv_buffer = lax.dynamic_update_slice(kv_buffer, added, (begin_row, zero_col))
        return (d_query_sum, kv_buffer)

    d_query_sum, kv_buffer = sweep_blocks(back_start, query_key_piece.shape[0], backward_step)
    kv_mine = lax.psum_scatter(
        kv_buffer.astype(jnp.bfloat16), "ctx", scatter_dimension=0, tiled=True
    ).astype(jnp.float32)
    d_kv = kv_mine.astype(bf16)
    d_queries = d_query_sum.reshape(local_rows, D).astype(bf16)
    d_stack = jnp.concatenate([d_queries, d_kv], axis=1)
    grad_qkv = contract_rows(normed_one, d_stack)
    grad_qv_b = jnp.stack(
        [jnp.sum(d_queries.astype(f32), axis=0), jnp.sum(d_kv[:, D : 2 * D].astype(f32), axis=0)]
    )
    d_norm_one = contract_cols(d_stack, full_qkv)
    unused_one, norm_back_one = jax.vjp(norm_apply, tokens, gain_one, bias_one)
    d_in_norm, grad_gain_one, grad_bias_one = norm_back_one(d_norm_one)
    grad_in = (d_resid + d_in_norm).astype(bf16)[None]
    attn_parts = (
        lax.psum_scatter(
            grad_gain_one.astype(jnp.bfloat16), "fsdp", scatter_dimension=0, tiled=True
        ).astype(jnp.float32),
        lax.psum_scatter(
            grad_bias_one.astype(jnp.bfloat16), "fsdp", scatter_dimension=0, tiled=True
        ).astype(jnp.float32),
        lax.psum_scatter(
            grad_qkv.astype(jnp.bfloat16), "fsdp", scatter_dimension=0, tiled=True
        ).astype(jnp.float32),
        lax.psum_scatter(
            grad_qv_b.astype(jnp.bfloat16), "fsdp", scatter_dimension=1, tiled=True
        ).astype(jnp.float32),
        lax.psum_scatter(
            grad_out.astype(jnp.bfloat16), "fsdp", scatter_dimension=0, tiled=True
        ).astype(jnp.float32),
        lax.psum_scatter(
            grad_out_b.astype(jnp.bfloat16), "fsdp", scatter_dimension=0, tiled=True
        ).astype(jnp.float32),
    )
    attn_parts = (
        lax.psum(attn_parts[0].astype(jnp.bfloat16), "ctx").astype(jnp.float32),
        lax.psum(attn_parts[1].astype(jnp.bfloat16), "ctx").astype(jnp.float32),
        lax.psum(attn_parts[2].astype(jnp.bfloat16), "ctx").astype(jnp.float32),
        lax.psum(attn_parts[3].astype(jnp.bfloat16), "ctx").astype(jnp.float32),
        lax.psum(attn_parts[4].astype(jnp.bfloat16), "ctx").astype(jnp.float32),
        lax.psum(attn_parts[5].astype(jnp.bfloat16), "ctx").astype(jnp.float32),
    )
    summed = (
        attn_parts[0],
        attn_parts[1],
        attn_parts[2],
        attn_parts[3],
        attn_parts[4],
        attn_parts[5],
        mlp_parts[0],
        mlp_parts[1],
        mlp_parts[2],
        mlp_parts[3],
        mlp_parts[4],
        mlp_parts[5],
    )
    return (
        layer_out,
        grad_in,
        summed[0],
        summed[1],
        summed[2],
        summed[3],
        summed[4],
        summed[5],
        summed[6],
        summed[7],
        summed[8],
        summed[9],
        summed[10],
        summed[11],
    )


def solution(mesh):
    placed = (
        P("fsdp", "ctx", None),
        P("fsdp", "ctx", None),
        P("fsdp"),
        P("fsdp"),
        P("fsdp", None),
        P(None, "fsdp"),
        P("fsdp", None),
        P("fsdp"),
        P("fsdp"),
        P("fsdp"),
        P("fsdp", None),
        P("fsdp"),
        P(None, "fsdp"),
        P("fsdp"),
    )
    return jax.shard_map(
        on_device,
        mesh=mesh,
        in_specs=placed,
        out_specs=(
            P("fsdp", "ctx", None),
            P("fsdp", "ctx", None),
            P("fsdp"),
            P("fsdp"),
            P("fsdp", None),
            P(None, "fsdp"),
            P("fsdp", None),
            P("fsdp"),
            P("fsdp"),
            P("fsdp"),
            P("fsdp", None),
            P("fsdp"),
            P(None, "fsdp"),
            P("fsdp"),
        ),
        check_vma=False,
    )
```

profile of v0, /device:TPU:0, one launch (start us, length us, event | category | flops | bytes accessed | tf_op | source)
XLA Modules:
  0.0 2621.7 jit_solution(15926004353740264351)
XLA Ops:
  10.0 13.5 all-gather
  25.2 28.7 %all-reduce.17 = (bf16[1600]{0:T(1024)(128)(2,1)S(1)}, bf16[1600]{0:T(1024)(128)(2,1)S(1)}, bf16[1600]{0:T(1024)(128)(2,1)S(1)}, bf16[6400]{0:T(1024)(128)(2,1)S...) all-reduce(bf16[1600]{0:T(1024)(128)(2,1)S(1)} %dynamic-update-slic, ...), channel_id=1, replica_groups=mesh['ctx'=8,'fsdp'=4] {'fsdp'}, use_global_device_ids=true, to_apply=%add.1 | all-reduce | flops 14400 | bytes 57600
  54.5 226.2 %all-gather.8.cloned.1.call-done = bf16[1600,4800]{1,0:T(8,128)(2,1)} async-done(((bf16[400,4800]{1,0:T(8,128)(2,1)}), bf16[1600,4800]{1,0:T(8,128)(2,1)}) %all-gather.8.cloned.1.call-update) | async-done | bytes 15360016 | tf_op jit(solution)/shard_map/all_gather | solution.py:72
  280.8 12.3 fusion.80
  299.8 27.8 %all-gather.12.cloned.1.call-done = bf16[1024,1600]{0,1:T(8,128)(2,1)} async-done(((bf16[128,1600]{0,1:T(8,128)(2,1)}), bf16[1024,1600]{0,1:T(8,128)(2,1)}) %all-gather.12.cloned.1.call-update) | async-done | bytes 3276816 | tf_op jit(solution)/shard_map/all_gather | solution.py:111
  327.6 35.9 %all-gather.10.cloned.1.call-done = bf16[1024,1600]{0,1:T(8,128)(2,1)} async-done(((bf16[128,1600]{0,1:T(8,128)(2,1)}), bf16[1024,1600]{0,1:T(8,128)(2,1)}) %all-gather.10.cloned.1.call-update) | async-done | bytes 3276816 | tf_op jit(solution)/shard_map/all_gather | solution.py:110
  363.5 20.6 while.34
  386.2 78.1 %all-gather.14.cloned.1.call-done = bf16[1600,1600]{1,0:T(8,128)(2,1)} async-done(((bf16[400,1600]{1,0:T(8,128)(2,1)}), bf16[1600,1600]{1,0:T(8,128)(2,1)}) %all-gather.14.cloned.1.call-update) | async-done | bytes 5120016 | tf_op jit(solution)/shard_map/all_gather | solution.py:74
  469.4 343.6 %all-gather.16.cloned.1.call-done = bf16[1600,6400]{1,0:T(8,128)(2,1)} async-done(((bf16[400,6400]{1,0:T(8,128)(2,1)}), bf16[1600,6400]{1,0:T(8,128)(2,1)}) %all-gather.16.cloned.1.call-update) | async-done | bytes 20480016 | tf_op jit(solution)/shard_map/all_gather | solution.py:78
  813.0 12.3 convolution_add_fusion
  825.3 336.6 %all-gather.18.cloned.1.call-done = bf16[6400,1600]{0,1:T(8,128)(2,1)} async-done(((bf16[6400,400]{0,1:T(8,128)(2,1)}), bf16[6400,1600]{0,1:T(8,128)(2,1)}) %all-gather.18.cloned.1.call-update) | async-done | bytes 20480016 | tf_op jit(solution)/shard_map/all_gather | solution.py:80
  1161.9 13.8 fusion.89
  1175.8 13.0 multiply_reduce_fusion
  1198.2 38.6 %while.35 = (s32[]{:T(128)}, f32[128,25,64]{0,2,1:T(8,128)S(1)}, f32[1024,3200]{0,1:T(8,128)}, bf16[1024,1600]{0,1:T(8,128)(2,1)}, bf16[128,25,64]{0,2,1:T(8,128...) while((s32[]{:T(128)}, f32[128,25,64]{0,2,1:T(8,128)S(1)}, ...), condition=%wide.region_12.13_spmd.clone, body=%wide.region_11.12_spmd.clone.sunk | while | flops 1291739776 | bytes 84286680 | solution.py:42
  1260.2 56.5 %reduce-scatter.19.cloned.1.call-done = bf16[128,3200]{1,0:T(8,128)(2,1)} async-done(((bf16[1024,3200]{1,0:T(8,128)(2,1)}), bf16[128,3200]{1,0:T(8,128)(2,1)}) %reduce-scatter.19.cloned.1.call-update) | async-done | bytes 819216
  1327.9 11.7 convolution_convert_fusion
  1354.4 60.5 %reduce-scatter.13.cloned.1.call-done = bf16[400,1600]{1,0:T(8,128)(2,1)} async-done(((bf16[1600,1600]{1,0:T(8,128)(2,1)}), bf16[400,1600]{1,0:T(8,128)(2,1)}) %reduce-scatter.13.cloned.1.call-update) | async-done | bytes 1280016 | tf_op jit(solution)/shard_map/reduce_scatter | solution.py:265
  1414.9 263.4 %reduce-scatter.11.cloned.1.call-done = bf16[400,4800]{1,0:T(8,128)(2,1)} async-done(((bf16[1600,4800]{1,0:T(8,128)(2,1)}), bf16[400,4800]{1,0:T(8,128)(2,1)}) %reduce-scatter.11.cloned.1.call-update) | async-done | bytes 3840016 | tf_op jit(solution)/shard_map/reduce_scatter | solution.py:259
  1678.3 343.0 %reduce-scatter.17.cloned.1.call-done = bf16[6400,400]{0,1:T(8,128)(2,1)} async-done(((bf16[6400,1600]{0,1:T(8,128)(2,1)}), bf16[6400,400]{0,1:T(8,128)(2,1)}) %reduce-scatter.17.cloned.1.call-update) | async-done | bytes 5120016 | tf_op jit(solution)/shard_map/reduce_scatter | solution.py:172
  2021.2 343.3 %reduce-scatter.15.cloned.1.call-done = bf16[400,6400]{1,0:T(8,128)(2,1)} async-done(((bf16[1600,6400]{1,0:T(8,128)(2,1)}), bf16[400,6400]{1,0:T(8,128)(2,1)}) %reduce-scatter.15.cloned.1.call-update) | async-done | bytes 5120016 | tf_op jit(solution)/shard_map/reduce_scatter | solution.py:166
  2377.0 19.9 all-reduce.16
  2399.9 11.7 fusion.50
  2412.6 24.1 all-reduce.14
  2441.3 156.2 %all-reduce.20.cloned.1.call-done = (bf16[400,4800]{1,0:T(8,128)(2,1)}, bf16[400,1600]{1,0:T(8,128)(2,1)}, bf16[400,6400]{1,0:T(8,128)(2,1)}, bf16[6400,400]{0,1:T(8,128)(2,1)}) async-done(((bf16[400,4800]{1,0:T(8,128)(2,1)}, bf16[400,1600]{1,0:T(8,128)(2,1)}, bf16[400,6400]{1,0:T(8,128)(2,1)}, bf16[6400,400]{0,1:T(8,128)(2,1)}), (bf16[400,4800]{1,0:T(8,128)(2,1)}, bf16[400,1600]{1,0:T(8,128)(2,1)}, ...) | async-done | bytes 15360016 | tf_op jit(solution)/shard_map/psum | solution.py:275
  (273 shorter events, 171.7 us)
Async XLA Ops:
  7.3 273.5 %all-gather.8.cloned.1.call-start = ((), (), s32[]{:S(2)}) async-start(), calls=%async_computation.6 | async-start | bytes 19456000 | tf_op jit(solution)/shard_map/all_gather | solution.py:72
  8.0 319.6 %all-gather.12.cloned.1.call-start = ((), (), s32[]{:S(2)}) async-start(), calls=%async_computation.8 | async-start | bytes 3686400 | tf_op jit(solution)/shard_map/all_gather | solution.py:111
  54.0 239.1 %copy-start.26 = (f32[1600]{0:T(1024)}, f32[1600]{0:T(1024)S(1)}, u32[]{:S(2)}) copy-start(f32[1600]{0:T(1024)S(1)} %convert_element_type.234) | copy-start | bytes 19204
  54.0 239.1 %copy-start.22 = (f32[1600]{0:T(1024)}, f32[1600]{0:T(1024)S(1)}, u32[]{:S(2)}) copy-start(f32[1600]{0:T(1024)S(1)} %convert_element_type.233) | copy-start | bytes 19204
  54.3 238.8 %copy-start.32 = (f32[128]{0:T(128)}, f32[128]{0:T(128)S(1)}, u32[]{:S(2)}) copy-start(f32[128]{0:T(128)S(1)} %broadcast_multiply_fusion.1) | copy-start | bytes 1540
  54.5 238.5 %copy-start.51 = (f32[128]{0:T(128)}, f32[128]{0:T(128)S(1)}, u32[]{:S(2)}) copy-start(f32[128]{0:T(128)S(1)} %fusion.61) | copy-start | bytes 1540
  54.5 238.5 %copy-start.38 = (f32[128]{0:T(128)}, f32[128]{0:T(128)S(1)}, u32[]{:S(2)}) copy-start(f32[128]{0:T(128)S(1)} %fusion.75) | copy-start | bytes 1540
  295.7 67.7 %all-gather.10.cloned.1.call-start = ((), (), s32[]{:S(2)}) async-start(), calls=%async_computation.7 | async-start | bytes 3686400 | tf_op jit(solution)/shard_map/all_gather | solution.py:110
  297.7 166.6 %all-gather.14.cloned.1.call-start = ((), (), s32[]{:S(2)}) async-start(), calls=%async_computation.9 | async-start | bytes 6656000 | tf_op jit(solution)/shard_map/all_gather | solution.py:74
  298.3 514.7 %all-gather.16.cloned.1.call-start = ((), (), s32[]{:S(2)}) async-start(), calls=%async_computation.10 | async-start | bytes 25600000 | tf_op jit(solution)/shard_map/all_gather | solution.py:78
  298.9 863.0 %all-gather.18.cloned.1.call-start = ((), (), s32[]{:S(2)}) async-start(), calls=%async_computation.11 | async-start | bytes 25600000 | tf_op jit(solution)/shard_map/all_gather | solution.py:80
  299.5 1017.2 %reduce-scatter.19.cloned.1.call-start = ((), (), s32[]{:S(2)}) async-start(), calls=%async_computation.16 | async-start | bytes 7372800
  299.8 889.0 %copy-start.20 = (f32[1600]{0:T(1024)}, f32[1600]{0:T(1024)S(1)}, u32[]{:S(2)}) copy-start(f32[1600]{0:T(1024)S(1)} %convert_element_type.242) | copy-start | bytes 19204
  299.8 513.2 %copy-start.24 = (f32[1600]{0:T(1024)}, f32[1600]{0:T(1024)S(1)}, u32[]{:S(2)}) copy-start(f32[1600]{0:T(1024)S(1)} %convert_element_type.243) | copy-start | bytes 19204
  469.1 719.7 %copy-start = (f32[128,1600]{0,1:T(8,128)}, f32[128,1600]{0,1:T(8,128)S(1)}, u32[]{:S(2)}) copy-start(f32[128,1600]{0,1:T(8,128)S(1)} %get-tuple-element.486) | copy-start | bytes 2457604
  469.1 719.7 %copy-start.28 = (f32[128]{0:T(128)}, f32[128]{0:T(128)S(1)}, u32[]{:S(2)}) copy-start(f32[128]{0:T(128)S(1)} %broadcast_multiply_fusion) | copy-start | bytes 1540
  469.4 719.4 %copy-start.30 = (f32[128]{0:T(128)}, f32[128]{0:T(128)S(1)}, u32[]{:S(2)}) copy-start(f32[128]{0:T(128)S(1)} %fusion.76) | copy-start | bytes 1540
  469.4 692.5 %copy-start.6 = (bf16[1,128,1600]{1,2,0:T(8,128)(2,1)S(1)}, bf16[1,128,1600]{1,2,0:T(8,128)(2,1)}, u32[]{:S(2)}) copy-start(bf16[1,128,1600]{1,2,0:T(8,128)(2,1)} %param.19) | copy-start | bytes 1228804
  1254.9 160.0 %reduce-scatter.13.cloned.1.call-start = ((), (), s32[]{:S(2)}) async-start(), calls=%async_computation.13 | async-start | bytes 6656000 | tf_op jit(solution)/shard_map/reduce_scatter | solution.py:265
  1259.8 418.4 %reduce-scatter.11.cloned.1.call-start = ((), (), s32[]{:S(2)}) async-start(), calls=%async_computation.12 | async-start | bytes 19456000 | tf_op jit(solution)/shard_map/reduce_scatter | solution.py:259
  1326.9 694.3 %reduce-scatter.17.cloned.1.call-start = ((), (), s32[]{:S(2)}) async-start(), calls=%async_computation.15 | async-start | bytes 25600000 | tf_op jit(solution)/shard_map/reduce_scatter | solution.py:172
  1339.7 1024.8 %reduce-scatter.15.cloned.1.call-start = ((), (), s32[]{:S(2)}) async-start(), calls=%async_computation.14 | async-start | bytes 25600000 | tf_op jit(solution)/shard_map/reduce_scatter | solution.py:166
  1351.8 1059.8 %reduce-scatter.21.cloned.1.call-start = ((), (), s32[]{:S(2)}) async-start(), calls=%async_computation.17 | async-start | bytes 512000
  1354.2 1243.4 %all-reduce.20.cloned.1.call-start = ((), (), s32[]{:S(2)}) async-start(), calls=%async_computation.18 | async-start | bytes 30924800 | tf_op jit(solution)/shard_map/psum | solution.py:275
  (46 other events, 802.9 us)
Sparse Core Ops, SparseCore 0:
  9.7 271.0 all-gather.7
  295.8 31.6 all-gather.11
  330.0 33.3 all-gather.9
  364.9 99.4 all-gather.13
  465.8 347.1 all-gather.15
  814.4 347.4 all-gather.17
  1255.0 61.5 reduce-scatter.18
  1319.6 95.2 reduce-scatter.12
  1417.4 260.8 reduce-scatter.10
  1680.5 340.6 reduce-scatter.16
  2023.7 340.7 reduce-scatter.14
  2367.2 22.1 reduce-scatter.20
  2394.0 203.5 all-reduce.19
where the time goes:
time: 2630 us; the launch traced here: 2620 us
  waiting for transfers between devices  2270 us (86%)
  matrix products  145 us (6%)
  blocking collectives  86.2 us (3%)
  other arithmetic  58.3 us (2%)
  local copies, waits for them, and re-layouts  39.9 us (2%)
    all_gather x1, waiting for transfers between devices, on_device(): lax.all_gather(fc_weight, 'fsdp', axis=0, tiled=True)  344 us
    reduce_scatter x1, waiting for transfers between devices, on_device(): lax.psum_scatter(grad_fc.astype(jnp.bfloat16), 'fsdp', scatter_dimension=...  343 us
    reduce_scatter x1, waiting for transfers between devices, on_device(): lax.psum_scatter(grad_proj.astype(jnp.bfloat16), 'fsdp', scatter_dimensio...  343 us
    all_gather x1, waiting for transfers between devices, on_device(): lax.all_gather(proj_weight, 'fsdp', axis=1, tiled=True)  337 us
    reduce_scatter x1, waiting for transfers between devices, on_device(): lax.psum_scatter(grad_qkv.astype(jnp.bfloat16), 'fsdp', scatter_dimension...  263 us
    all_gather x1, waiting for transfers between devices, on_device(): lax.all_gather(qkv_weight, 'fsdp', axis=0, tiled=True)  226 us
    psum x1, waiting for transfers between devices, on_device(): lax.psum(attn_parts[2].astype(jnp.bfloat16), 'ctx').astype(jnp.float32)  156 us
    all_gather x1, waiting for transfers between devices, on_device(): lax.all_gather(out_weight, 'fsdp', axis=0, tiled=True)  78.1 us
  transfers between devices with their start and end apart: 13, of which 12 were waited for; matrix products, arithmetic and copies ran while one was open for 4% of the time, Pallas kernels for 0%

commit v1 on v0

v1 whole, which is shorter than its diff:
```python
import math

import jax
import jax.numpy as jnp
from jax import lax
from jax.experimental import pallas as pl
from jax.experimental.pallas import tpu as pltpu
from jax.sharding import PartitionSpec as P

H = 25
HD = 64
ROWS = 256

f32 = jnp.float32
bf16 = jnp.bfloat16


def norm_apply(values, norm_gain, norm_bias):
    centre = jnp.mean(values, axis=-1, keepdims=True)
    shifted = values - centre
    spread = jnp.mean(shifted * shifted, axis=-1, keepdims=True)
    return shifted * lax.rsqrt(spread + 1e-05) * norm_gain + norm_bias


def matmul(left, right, left_dim, right_dim):
    return lax.dot_general(
        left, right, (((left_dim,), (right_dim,)), ((), ())), preferred_element_type=f32
    )


class Plane:
    def __init__(self, size):
        self.size = size
        self.chips = size // 2
        self.wide = math.isqrt(self.chips)
        self.tall = self.chips // self.wide
        self.shifts = [(da, db) for da in range(self.tall) for db in range(self.wide)]
        self.me = lax.axis_index("ctx")

    def _moved(self, chip, shift, sign):
        row, col = chip // self.wide, chip % self.wide
        row = (row + sign * shift[0] + self.tall) % self.tall
        col = (col + sign * shift[1] + self.wide) % self.wide
        return row * self.wide + col

    def index_of(self, slot):
        core = self.me % 2
        if slot >= self.chips:
            core = 1 - core
        return self._moved(self.me // 2, self.shifts[slot % self.chips], -1) * 2 + core

    def from_slot(self, value, slot):
        return lax.ppermute(value, "ctx", self._pairs(slot, 1))

    def to_slot(self, value, slot):
        return lax.ppermute(value, "ctx", self._pairs(slot, -1))

    def _pairs(self, slot, sign):
        shift, flip = self.shifts[slot % self.chips], slot // self.chips
        return [
            (i, self._moved(i // 2, shift, sign) * 2 + (i % 2 + flip) % 2)
            for i in range(self.size)
        ]

    def opposite(self, slot):
        da, db = self.shifts[slot % self.chips]
        shift = ((self.tall - da) % self.tall, (self.wide - db) % self.wide)
        return self.shifts.index(shift) + self.chips * (slot // self.chips)

    def swap(self, value):
        return self.to_slot(value, self.chips)

    def gather(self, value):
        mine = jnp.concatenate(
            [value] + [self.from_slot(value, slot) for slot in range(1, self.chips)], axis=0
        )
        return jnp.concatenate([mine, self.swap(mine)], axis=0)

    def scatter(self, mine, theirs):
        total = mine + self.swap(theirs.astype(bf16)).astype(f32)
        total = total.reshape((self.chips, -1) + mine.shape[1:])
        sent = total[1:].astype(bf16)
        result = total[0]
        for slot in range(1, self.chips):
            result = result + self.to_slot(sent[slot - 1], slot).astype(f32)
        return result


def line_gather(value, size):
    at = lax.axis_index("fsdp")
    rows = value.shape[0]
    zeros = (0,) * (value.ndim - 1)

    def put(whole, part, block):
        return lax.dynamic_update_slice(whole, part, (block * rows,) + zeros)

    whole = jnp.zeros((size * rows,) + value.shape[1:], value.dtype)
    if size != 4:
        whole = put(whole, value, at)
        for step in range(1, size):
            moved = lax.ppermute(value, "fsdp", [(i, (i + step) % size) for i in range(size)])
            whole = put(whole, moved, (at - step) % size)
        return whole
    up = lax.ppermute(value, "fsdp", [(0, 1), (1, 2), (2, 3)])
    down = lax.ppermute(value, "fsdp", [(1, 0), (2, 1), (3, 2)])
    cross = lax.ppermute(value, "fsdp", [(0, 2), (1, 3), (2, 0), (3, 1)])
    relay = lax.ppermute(cross, "fsdp", [(2, 3), (1, 0)])
    whole = put(whole, up, (at + 3) % 4)
    whole = put(whole, down, (at + 1) % 4)
    whole = put(whole, cross, (at + 2) % 4)
    whole = put(whole, relay, jnp.where(at == 0, 3, jnp.where(at == 3, 0, at)))
    return put(whole, value, at)


def line_scatter(parts, size):
    at = lax.axis_index("fsdp")

    def part(block):
        return lax.dynamic_index_in_dim(parts, block % size, 0, keepdims=False)

    result = part(at)
    if size != 4:
        for step in range(1, size):
            moved = lax.ppermute(
                part(at + step).astype(bf16), "fsdp", [(i, (i + step) % size) for i in range(size)]
            )
            result = result + moved.astype(f32)
        return result
    relay = lax.ppermute(part(3 - at).astype(bf16), "fsdp", [(0, 1), (3, 2)])
    up = lax.ppermute(part(at + 1).astype(bf16), "fsdp", [(0, 1), (1, 2), (2, 3)])
    down = lax.ppermute(part(at + 3).astype(bf16), "fsdp", [(1, 0), (2, 1), (3, 2)])
    cross = part(at + 2) + relay.astype(f32)
    cross = lax.ppermute(cross.astype(bf16), "fsdp", [(0, 2), (1, 3), (2, 0), (3, 1)])
    return result + up.astype(f32) + down.astype(f32) + cross.astype(f32)


def _blocks(length):
    count = length // ROWS
    return count, count <= 4


def _scores_t(key_head, query_block, first, length):
    scores = matmul(key_head, query_block, 1, 1)
    key_at = lax.broadcasted_iota(jnp.int32, scores.shape, 0)
    query_at = lax.broadcasted_iota(jnp.int32, scores.shape, 1) + first
    return scores, key_at <= query_at


def forward_kernel(heads, places, q_ref, k_ref, v_ref, out_ref, out_t_ref, log_ref, q_s, k_s, v_s):
    length = q_ref.shape[0]
    slots = places.shape[0]
    rows = length // slots
    for slot in range(slots):
        to = pl.ds(pl.multiple_of(places[slot] * rows, rows), rows)
        at = pl.ds(slot * rows, rows)
        q_s[to, :] = q_ref[at, :]
        k_s[to, :] = k_ref[at, :]
        v_s[to, :] = v_ref[at, :]

    count, few = _blocks(length)
    for head in range(heads):
        cols = slice(head * HD, (head + 1) * HD)

        def block(index, head=head, cols=cols):
            first = index * ROWS
            until = first + ROWS if few else length
            query = q_s[pl.ds(first, ROWS), cols]
            scores, kept = _scores_t(k_s[0:until, cols], query, first, length)
            scores = jnp.where(kept, scores, -1e30)
            top = jnp.max(scores, axis=0, keepdims=True)
            weights = jnp.exp(scores - top)
            total = jnp.sum(weights, axis=0, keepdims=True)
            summed = matmul(v_s[0:until, cols].T, weights.astype(bf16), 1, 0)
            out_t_ref[cols, pl.ds(first, ROWS)] = summed / total
            log_ref[head : head + 1, pl.ds(first, ROWS)] = top + jnp.log(total)

        if few:
            for index in range(count):
                block(index)
        else:
            lax.fori_loop(0, count, lambda i, c: (block(i), c)[1], 0)
    q_s[...] = out_t_ref[...].T.astype(bf16)
    for slot in range(slots):
        to = pl.ds(pl.multiple_of(places[slot] * rows, rows), rows)
        out_ref[pl.ds(slot * rows, rows), :] = q_s[to, :]


def backward_kernel(
    heads, places, q_ref, k_ref, v_ref, d_ref, out_t_ref, log_ref, g_ref,
    q_s, k_s, v_s, d_s, dk_s, dv_s, dq_t
):
    length = q_ref.shape[0]
    slots = places.shape[0]
    rows = length // slots
    width = heads * HD
    for slot in range(slots):
        to = pl.ds(pl.multiple_of(places[slot] * rows, rows), rows)
        at = pl.ds(slot * rows, rows)
        q_s[to, :] = q_ref[at, :]
        k_s[to, :] = k_ref[at, :]
        v_s[to, :] = v_ref[at, :]
        d_s[to, :] = d_ref[at, :]
    dk_s[...] = jnp.zeros_like(dk_s)
    dv_s[...] = jnp.zeros_like(dv_s)
    count, few = _blocks(length)
    for head in range(heads):
        cols = slice(head * HD, (head + 1) * HD)

        def block(index, head=head, cols=cols):
            first = index * ROWS
            until = first + ROWS if few else length
            at = pl.ds(first, ROWS)
            query = q_s[at, cols]
            cot = d_s[at, cols]
            delta = jnp.sum(cot.astype(f32).T * out_t_ref[cols, at], axis=0, keepdims=True)
            scores, kept = _scores_t(k_s[0:until, cols], query, first, length)
            weights = jnp.where(kept, jnp.exp(scores - log_ref[head : head + 1, at]), 0.0)
            d_weights = matmul(v_s[0:until, cols], cot, 1, 1)
            d_scores = (weights * (d_weights - delta)).astype(bf16)
            dv_s[head, 0:until, :] += matmul(weights.astype(bf16), cot, 1, 0)
            dk_s[head, 0:until, :] += matmul(d_scores, query, 1, 0)
            dq_t[cols, at] = matmul(k_s[0:until, cols].T, d_scores, 1, 0)

        if few:
            for index in range(count):
                block(index)
        else:
            lax.fori_loop(0, count, lambda i, c: (block(i), c)[1], 0)
    scale = 1.0 / math.sqrt(HD)
    q_s[...] = (dq_t[...] * scale).T.astype(bf16)
    for head in range(heads):
        cols = slice(head * HD, (head + 1) * HD)
        k_s[:, cols] = dk_s[head].astype(bf16)
        v_s[:, cols] = dv_s[head].astype(bf16)
    for slot in range(slots):
        to = pl.ds(pl.multiple_of(places[slot] * rows, rows), rows)
        at = pl.ds(slot * rows, rows)
        g_ref[at, 0:width] = q_s[to, :]
        g_ref[at, width : 2 * width] = k_s[to, :]
        g_ref[at, 2 * width : 3 * width] = v_s[to, :]


VMEM = pl.BlockSpec(memory_space=pltpu.VMEM)
SMEM = pl.BlockSpec(memory_space=pltpu.SMEM)


def attend(heads, places, query, key, value):
    length, width = query.shape
    return pl.pallas_call(
        lambda *refs: forward_kernel(heads, *refs),
        out_shape=(
            jax.ShapeDtypeStruct((length, width), bf16),
            jax.ShapeDtypeStruct((width, length), f32),
            jax.ShapeDtypeStruct((heads, length), f32),
        ),
        in_specs=[SMEM, VMEM, VMEM, VMEM],
        out_specs=(VMEM, VMEM, VMEM),
        scratch_shapes=[pltpu.VMEM((length, width), bf16)] * 3,
        name="attend",
    )(places, query, key, value)


def attend_back(heads, places, query, key, value, cot, out_t, log_total):
    length, width = query.shape
    return pl.pallas_call(
        lambda *refs: backward_kernel(heads, *refs),
        out_shape=jax.ShapeDtypeStruct((length, 3 * width), bf16),
        in_specs=[SMEM] + [VMEM] * 6,
        out_specs=VMEM,
        scratch_shapes=[pltpu.VMEM((length, width), bf16)] * 4
        + [pltpu.VMEM((heads, length, HD), f32)] * 2
        + [pltpu.VMEM((width, length), f32)],
        name="attend_back",
    )(places, query, key, value, cot, out_t, log_total)


def on_device(
    layer_in, out_cot, first_gain, first_bias, qkv_weight, qv_bias, out_weight, out_bias,
    second_gain, second_bias, fc_weight, fc_bias, proj_weight, proj_bias
):
    size = lax.axis_size("ctx")
    line = lax.axis_size("fsdp")
    plane = Plane(size)
    me = plane.me
    tokens = layer_in[0].astype(f32)
    rows, width = tokens.shape
    piece = width // line
    hidden = fc_weight.shape[1]
    part = hidden // size
    heads = -(-H // size)
    span = heads * HD
    spread = size * span
    share = -(-(-(-piece // size)) // 8) * 8
    slots = range(size)
    places = jnp.stack([plane.index_of(slot) for slot in slots]).astype(jnp.int32)
    slot_of = [0] * size
    order = jnp.zeros((size,), jnp.int32)
    order = order.at[places].set(jnp.arange(size, dtype=jnp.int32))

    vectors = jnp.concatenate(
        [
            first_gain[None], first_bias[None], qv_bias, out_bias[None], second_gain[None],
            second_bias[None], proj_bias[None], fc_bias.reshape(-1, piece),
        ],
        axis=0,
    )
    count = vectors.shape[0]
    vectors = line_gather(vectors, line).reshape(line, count, piece).astype(f32)
    gain_one, bias_one, bias_q, bias_v, bias_out, gain_two, bias_two, bias_proj = (
        vectors[:, i].reshape(width) for i in range(8)
    )
    bias_fc = vectors[:, 8:].reshape(hidden)
    bias_fc = lax.dynamic_slice_in_dim(bias_fc, me * part, part)

    def heads_of(vector):
        padded = jnp.pad(vector, ((0, spread - width),))
        return lax.dynamic_slice_in_dim(padded, me * span, span)

    padded = jnp.pad(qkv_weight, ((0, 0), (0, spread - width)))
    own_qkv = jnp.concatenate(
        [
            lax.dynamic_slice_in_dim(padded, i * width + me * span, span, axis=1)
            for i in range(3)
        ],
        axis=1,
    )
    full_qkv = line_gather(own_qkv, line)
    padded = jnp.pad(out_weight, ((0, size * share - piece), (0, 0)))
    own_out = lax.dynamic_slice_in_dim(padded, me * share, share, axis=0)
    all_out = line_gather(own_out, line)
    own_fc = lax.dynamic_slice_in_dim(fc_weight, me * part, part, axis=1)
    full_fc = line_gather(own_fc, line)
    own_proj = lax.dynamic_slice_in_dim(proj_weight, me * part, part, axis=0).T
    full_proj = line_gather(own_proj, line)

    normed_one = norm_apply(tokens, gain_one, bias_one).astype(bf16)
    normed_one = plane.gather(normed_one)
    projected = matmul(normed_one, full_qkv, 1, 0)
    scale = 1.0 / math.sqrt(HD)
    queries = (projected[:, 0:span] + heads_of(bias_q)).astype(bf16) * jnp.asarray(scale, bf16)
    keys = projected[:, span : 2 * span].astype(bf16)
    values = (projected[:, 2 * span :] + heads_of(bias_v)).astype(bf16)
    attn_heads, attn_t, log_total = attend(heads, places, queries, keys, values)

    def to_tokens(by_slot):
        got = [None] * size
        got[0] = by_slot[0]
        for slot in range(1, size):
            got[plane.opposite(slot)] = plane.to_slot(by_slot[slot], slot)
        got = jnp.stack(got)
        got = [lax.dynamic_index_in_dim(got, order[i], 0, keepdims=False) for i in range(size)]
        return jnp.concatenate(got, axis=1)[:, :width]

    def to_heads(by_token):
        by_token = jnp.pad(by_token, ((0, 0), (0, spread - width)))
        got = [None] * size
        for slot in range(size):
            block = lax.dynamic_slice_in_dim(by_token, places[slot] * span, span, axis=1)
            got[plane.opposite(slot)] = plane.to_slot(block, slot) if slot else block
        return jnp.concatenate(got, axis=0)

    attn_out = to_tokens(attn_heads.reshape(size, rows, span))
    all_out = plane.gather(all_out[None])
    all_out = jnp.concatenate(
        [
            lax.dynamic_index_in_dim(all_out, order[i], 0).reshape(line, share, width)
            for i in range(size)
        ],
        axis=1,
    )
    full_out = all_out[:, :piece].reshape(width, width)
    resid = tokens + matmul(attn_out, full_out, 1, 0) + bias_out

    cotangent = out_cot[0]
    all_cot = plane.gather(cotangent)
    normed_two = norm_apply(resid, gain_two, bias_two).astype(bf16)
    normed_two = plane.gather(normed_two)
    pre_act = matmul(normed_two, full_fc, 1, 0) + bias_fc
    activated, gelu_back = jax.vjp(lambda v: jax.nn.gelu(v, approximate=True), pre_act)
    activated = activated.astype(bf16)
    half = size // 2 * rows
    mlp_theirs = matmul(activated[half:], full_proj, 1, 1)
    mlp_mine = matmul(activated[:half], full_proj, 1, 1)
    d_activated = matmul(all_cot, full_proj, 1, 0)
    d_pre = gelu_back(d_activated)[0].astype(bf16)
    norm_theirs = matmul(d_pre[half:], full_fc, 1, 1)
    norm_mine = matmul(d_pre[:half], full_fc, 1, 1)
    d_norm_two = plane.scatter(norm_mine, norm_theirs)
    grad_proj = matmul(all_cot, activated, 0, 0).reshape(line, piece, part)
    grad_fc = matmul(normed_two, d_pre, 0, 0).reshape(line, piece, part)
    layer_out = plane.scatter(mlp_mine, mlp_theirs) + resid + bias_proj
    layer_out = layer_out.astype(bf16)[None]

    unused_two, norm_back_two = jax.vjp(norm_apply, resid, gain_two, bias_two)
    d_resid_norm, grad_gain_two, grad_bias_two = norm_back_two(d_norm_two)
    cot_float = cotangent.astype(f32)
    d_resid = cot_float + d_resid_norm
    d_branch = d_resid.astype(bf16)

    d_attn = matmul(d_branch, full_out, 1, 1).astype(bf16)
    d_attn = to_heads(d_attn)
    grads = attend_back(heads, places, queries, keys, values, d_attn, attn_t, log_total)
    grad_qkv = matmul(normed_one, grads, 0, 0).reshape(line, piece, 3 * span)
    d_theirs = matmul(grads[half:], full_qkv, 1, 1)
    d_mine = matmul(grads[:half], full_qkv, 1, 1)
    d_norm_one = plane.scatter(d_mine, d_theirs)
    unused_one, norm_back_one = jax.vjp(norm_apply, tokens, gain_one, bias_one)
    d_in_norm, grad_gain_one, grad_bias_one = norm_back_one(d_norm_one)
    grad_in = (d_resid + d_in_norm).astype(bf16)[None]

    def spread_out(value):
        value = plane.gather(value.astype(bf16)[None])
        return [lax.dynamic_index_in_dim(value, order[i], 0, keepdims=False) for i in range(size)]

    grad_proj = spread_out(line_scatter(grad_proj, line).T)
    grad_proj = jnp.concatenate(grad_proj, axis=0).astype(f32)
    grad_fc = spread_out(line_scatter(grad_fc, line))
    grad_fc = jnp.concatenate(grad_fc, axis=1).astype(f32)
    grad_qkv = spread_out(line_scatter(grad_qkv, line))
    grad_qkv = jnp.concatenate(
        [
            jnp.concatenate([g[:, i * span : (i + 1) * span] for g in grad_qkv], axis=1)[:, :width]
            for i in range(3)
        ],
        axis=1,
    ).astype(f32)

    grad_out = matmul(attn_out, d_branch, 0, 0).reshape(line, piece, width)
    grad_out = jnp.pad(grad_out, ((0, 0), (0, size * share - piece), (0, 0)))
    grad_out = grad_out.reshape(line, size, share, width)
    by_slot = [
        lax.dynamic_index_in_dim(grad_out, places[i], 1, keepdims=False) for i in range(size)
    ]
    mine = jnp.concatenate(by_slot[: size // 2], axis=0).reshape(size // 2 * line * share, width)
    theirs = jnp.concatenate(by_slot[size // 2 :], axis=0).reshape(mine.shape)
    grad_out = plane.scatter(mine, theirs).reshape(line, share, width)
    grad_out = spread_out(line_scatter(grad_out, line))
    grad_out = jnp.concatenate(grad_out, axis=0)[:piece].astype(f32)

    def summed(value):
        return jnp.sum(value.astype(f32), axis=0)

    vectors = jnp.concatenate(
        [
            grad_gain_one, grad_bias_one, summed(d_branch), grad_gain_two, grad_bias_two,
            summed(cot_float), summed(grads[:, :span]), summed(grads[:, 2 * span :]),
            summed(d_pre),
        ]
    )
    vectors = plane.gather(vectors[None])
    by_token = jnp.sum(vectors[:, : 6 * width], axis=0).reshape(6, line, piece)
    vectors = jnp.take(vectors, order, axis=0)[:, 6 * width :]
    bias_parts = jnp.stack(
        [vectors[:, i * span : (i + 1) * span].reshape(spread)[:width] for i in range(2)]
    ).reshape(2, line, piece)
    hidden_part = vectors[:, 2 * span :].reshape(line, hidden // line)
    parts = jnp.concatenate(
        [
            by_token.transpose(1, 0, 2).reshape(line, 6 * piece),
            bias_parts.transpose(1, 0, 2).reshape(line, 2 * piece),
            hidden_part,
        ],
        axis=1,
    )
    final = line_scatter(parts, line)
    singles = [final[i * piece : (i + 1) * piece] for i in range(8)]
    return (
        layer_out,
        grad_in,
        singles[0],
        singles[1],
        grad_qkv,
        jnp.stack(singles[6:8]),
        grad_out,
        singles[2],
        singles[3],
        singles[4],
        grad_fc,
        final[8 * piece :],
        grad_proj,
        singles[5],
    )


def solution(mesh):
    by_width = P("fsdp")
    tokens = P("fsdp", "ctx", None)
    matrix = P("fsdp", None)
    across = P(None, "fsdp")
    params = (
        by_width, by_width, matrix, across, matrix, by_width, by_width, by_width, matrix, by_width,
        across, by_width,
    )
    return jax.shard_map(
        on_device,
        mesh=mesh,
        in_specs=(tokens, tokens) + params,
        out_specs=(tokens, tokens) + params,
        check_vma=False,
    )
```

time: 2630 us -> 847 us (0.32)
  waiting for transfers between devices: 2270 us -> 346 us
  starting transfers between devices: 1.28 us -> 189 us
  local copies, waits for them, and re-layouts: 39.9 us -> 135 us
  matrix products: 145 us -> 57.1 us
  blocking collectives: 86.2 us -> 0 us
    all_gather x6 -> x0, waiting for transfers between devices: 1050 us -> none  [the longest x1 344 us: on_device(): lax.all_gather(fc_weight, 'fsdp', axis=0, tiled=True)]
    reduce_scatter x4 -> x0, waiting for transfers between devices: 1010 us -> none  [the longest x1 343 us: on_device(): lax.psum_scatter(grad_fc.astype(jnp.bfloat16), 'fsdp', scatter_dimension=...]
    ppermute x0 -> x106, waiting for transfers between devices: none -> 346 us  [the longest x39 87.1 us: to_slot(): return lax.ppermute(value, 'ctx', self._pairs(slot, -1))]
    ppermute x0 -> x106, starting transfers between devices: none -> 189 us  [the longest x27 33.1 us: from_slot(): return lax.ppermute(value, 'ctx', self._pairs(slot, 1))]
    psum x1 -> x0, waiting for transfers between devices: 156 us -> none  [on_device(): lax.psum(attn_parts[2].astype(jnp.bfloat16), 'ctx').astype(jnp.float32)]
    dot_general x30 -> x15, matrix products: 145 us -> 57.1 us  [matmul(): lax.dot_general(left, right, (((left_dim,), (right_dim,)), ((), ())), pre...]
    unnamed x15 -> x0, waiting for transfers between devices: 58.9 us -> none
    unnamed x2 -> x0, blocking collectives: 48.6 us -> none
  transfers between devices with their start and end apart: 13 -> 106, of which waited for: 12 -> 43; matrix products, arithmetic and copies ran while one was open for 4% -> 26% of each run, Pallas kernels for 0% -> 1%
where the time goes in v1:
time: 847 us; the launch traced here: 837 us
  waiting for transfers between devices  346 us (41%)
  starting transfers between devices  189 us (22%)
  local copies, waits for them, and re-layouts  135 us (16%)
  other arithmetic  71 us (8%)
  matrix products  57.1 us (7%)
  Pallas kernels  20.6 us (2%)
  between operations  18.3 us (2%)
    ppermute x39, waiting for transfers between devices, to_slot(): return lax.ppermute(value, 'ctx', self._pairs(slot, -1))  87.1 us
    ppermute x27, waiting for transfers between devices, from_slot(): return lax.ppermute(value, 'ctx', self._pairs(slot, 1))  77.4 us
    ppermute x5, waiting for transfers between devices, line_scatter(): lax.ppermute(cross.astype(bf16), 'fsdp', [(0, 2), (1, 3), (2, 0), (3, 1)])  62.9 us
    dot_general x15, matrix products, matmul(): lax.dot_general(left, right, (((left_dim,), (right_dim,)), ((), ())), pre...  57.1 us
    ppermute x5, waiting for transfers between devices, line_gather(): relay = lax.ppermute(cross, 'fsdp', [(2, 3), (1, 0)])  55.1 us
    ppermute x27, starting transfers between devices, from_slot(): return lax.ppermute(value, 'ctx', self._pairs(slot, 1))  33.1 us
    ppermute x5, waiting for transfers between devices, line_gather(): cross = lax.ppermute(value, 'fsdp', [(0, 2), (1, 3), (2, 0), (3, 1)])  28.9 us
    ppermute x5, starting transfers between devices, line_gather(): cross = lax.ppermute(value, 'fsdp', [(0, 2), (1, 3), (2, 0), (3, 1)])  28.6 us
  transfers between devices with their start and end apart: 106, of which 43 were waited for; matrix products, arithmetic and copies ran while one was open for 26% of the time, Pallas kernels for 1%

profile of v1, /device:TPU:0, one launch (start us, length us, event | category | flops | bytes accessed | tf_op | source)
XLA Modules:
  0.0 837.2 jit_solution(2104130892581630657)
XLA Ops:
  68.4 10.7 %collective-permute-done.22 = bf16[56,1600]{1,0:T(8,128)(2,1)S(1)} collective-permute-done((bf16[56,1600]{1,0:T(8,128)(2,1)}, bf16[56,1600]{1,0:T(8,128)(2,1)S(1)}, u32[]{:S(2)}, u32[]{:S(2)}) %collective-permute-start.22) | collective-permute-done | bytes 179232 | tf_op jit(solution)/shard_map/ppermute | solution.py:107
  84.4 8.0 collective-permute-done.45
  113.1 12.1 %collective-permute-done.10 = bf16[400,768]{1,0:T(8,128)(2,1)S(1)} collective-permute-done((bf16[400,768]{1,0:T(8,128)(2,1)S(1)}, bf16[400,768]{1,0:T(8,128)(2,1)S(1)}, u32[]{:S(2)}, u32[]{:S(2)}) %collective-permute-start.10) | collective-permute-done | bytes 614432 | tf_op jit(solution)/shard_map/ppermute | solution.py:106
  128.4 14.5 %collective-permute-start.33 = (bf16[400,800]{1,0:T(8,128)(2,1)}, bf16[400,800]{1,0:T(8,128)(2,1)}, u32[]{:S(2)}, u32[]{:S(2)}) collective-permute-start(bf16[400,800]{1,0:T(8,128)(2,1)} %constant_dynamic-slice_fusion.5), channel_id=1, source_target_pairs={{0,2},{1,3},{2,0},{3,1},{4,6},{5,7},{6,4},{7,5},{8,10},{9,11},{10,... | collective-permute-start | bytes 1920008 | tf_op jit(solution)/shard_map/ppermute | solution.py:106
  154.0 16.5 %collective-permute-done.11 = bf16[400,768]{1,0:T(8,128)(2,1)S(1)} collective-permute-done((bf16[400,768]{1,0:T(8,128)(2,1)S(1)}, bf16[400,768]{1,0:T(8,128)(2,1)S(1)}, u32[]{:S(2)}, u32[]{:S(2)}) %collective-permute-start.11) | collective-permute-done | bytes 614432 | tf_op jit(solution)/shard_map/ppermute | solution.py:107
  176.2 9.3 %attend.1 = (bf16[1024,256]{1,0:T(8,128)(2,1)}, f32[256,1024]{1,0:T(8,128)}, f32[4,1024]{1,0:T(4,128)}) custom-call(s32[8]{0:T(128)} %stack.95.refs_0_, bf16[1024,256]{1,0:T(8,128)(2,1)} %get-tuple-element.117.refs_1_, bf16[1024,256]{1,0:T(8,128)(2,1)} %get-tuple-element.116.refs_2_, bf16[1024,256]{1,0:T(8,128)(2,1)} %fusion.22.refs_3_), custom_call_target="tpu_custom_call" | custom-call | tf_op jit(solution)/shard_map/attend/pallas_call | solution.py:249
  214.9 14.1 %collective-permute-start.36 = (bf16[400,800]{1,0:T(8,128)(2,1)}, bf16[400,800]{1,0:T(8,128)(2,1)}, u32[]{:S(2)}, u32[]{:S(2)}) collective-permute-start(bf16[400,800]{1,0:T(8,128)(2,1)} %dynamic-slice_bitcast_fusion.20), channel_id=1, source_target_pairs={{1,0},{2,1},{3,2},{5,4},{6,5},{7,6},{9,8},{10,9},{11,10},{13,12},{... | collective-permute-start | bytes 1920008 | tf_op jit(solution)/shard_map/ppermute | solution.py:105
  254.1 16.8 %collective-permute-done.37 = bf16[400,800]{1,0:T(8,128)(2,1)S(1)} collective-permute-done((bf16[400,800]{1,0:T(8,128)(2,1)}, bf16[400,800]{1,0:T(8,128)(2,1)S(1)}, u32[]{:S(2)}, u32[]{:S(2)}) %collective-permute-start.37) | collective-permute-done | bytes 640032 | tf_op jit(solution)/shard_map/ppermute | solution.py:106
  276.5 15.4 %collective-permute-done.34 = bf16[400,800]{1,0:T(8,128)(2,1)S(1)} collective-permute-done((bf16[400,800]{1,0:T(8,128)(2,1)}, bf16[400,800]{1,0:T(8,128)(2,1)S(1)}, u32[]{:S(2)}, u32[]{:S(2)}) %collective-permute-start.34) | collective-permute-done | bytes 640032 | tf_op jit(solution)/shard_map/ppermute | solution.py:107
  293.6 12.4 %collective-permute-done.38 = bf16[400,800]{1,0:T(8,128)(2,1)S(1)} collective-permute-done((bf16[400,800]{1,0:T(8,128)(2,1)S(1)}, bf16[400,800]{1,0:T(8,128)(2,1)S(1)}, u32[]{:S(2)}, u32[]{:S(2)}) %collective-permute-start.38) | collective-permute-done | bytes 640032 | tf_op jit(solution)/shard_map/ppermute | solution.py:107
  351.7 24.8 %collective-permute-done.100 = bf16[400,800]{1,0:T(8,128)(2,1)S(1)} collective-permute-done((bf16[400,800]{1,0:T(8,128)(2,1)S(1)}, bf16[400,800]{1,0:T(8,128)(2,1)S(1)}, u32[]{:S(2)}, u32[]{:S(2)}) %collective-permute-start.100) | collective-permute-done | bytes 640032 | tf_op jit(solution)/shard_map/ppermute | solution.py:129
  407.8 32.1 %collective-permute-done.101 = bf16[400,800]{1,0:T(8,128)(2,1)} collective-permute-done((bf16[400,800]{1,0:T(8,128)(2,1)}, bf16[400,800]{1,0:T(8,128)(2,1)}, u32[]{:S(2)}, u32[]{:S(2)}) %collective-permute-start.101) | collective-permute-done | bytes 640032 | tf_op jit(solution)/shard_map/ppermute | solution.py:133
  460.3 13.8 %collective-permute-done.102 = bf16[1,800,400]{1,2,0:T(8,128)(2,1)S(1)} collective-permute-done((bf16[1,800,400]{1,2,0:T(8,128)(2,1)S(1)}, bf16[1,800,400]{1,2,0:T(8,128)(2,1)S(1)}, u32[]{:S(2)}, u32[]{:S(2)}) %collective-permute-start.102) | collective-permute-done | bytes 640032 | tf_op jit(solution)/shard_map/ppermute | solution.py:53
  479.2 11.3 %collective-permute-done.104 = bf16[1,800,400]{1,2,0:T(8,128)(2,1)S(1)} collective-permute-done((bf16[1,800,400]{1,2,0:T(8,128)(2,1)S(1)}, bf16[1,800,400]{1,2,0:T(8,128)(2,1)S(1)}, u32[]{:S(2)}, u32[]{:S(2)}) %collective-permute-start.104) | collective-permute-done | bytes 640032 | tf_op jit(solution)/shard_map/ppermute | solution.py:53
  500.1 7.9 collective-permute-done.49
  508.9 8.0 collective-permute-done.42
  538.5 9.2 %pad.28 = f32[4,448,1600]{2,1,0:T(8,128)} pad(f32[4,400,1600]{2,1,0:T(8,128)} %bitcast.357, f32[]{:T(128)} %constant.478.clone.1), padding=0_0x0_48x0_0 | pad | bytes 21708804 | tf_op jit(solution)/shard_map/jit(_pad)/pad | solution.py:429
  559.3 11.3 %attend_back.1 = bf16[1024,768]{1,0:T(8,128)(2,1)} custom-call(s32[8]{0:T(128)} %stack.95.refs_0_, bf16[1024,256]{1,0:T(8,128)(2,1)} %get-tuple-element.117.refs_1_, bf16[1024,256]{1,0:T(8,128)(2,1)} %get-tuple-element.116.refs_2_, bf16[1024,256]{1,0:T(8,128)(2,1)} %fusion.22.refs_3_, bf16[1024,256]{1,0:T(8,128)(2,1)} %copy-done.32, ...), custom_call_target="tpu_custom_call" | custom-call | tf_op jit(solution)/shard_map/attend_back/pallas_call | solution.py:265
  611.6 17.2 %collective-permute-done.73 = bf16[400,768]{1,0:T(8,128)(2,1)} collective-permute-done((bf16[400,768]{1,0:T(8,128)(2,1)}, bf16[400,768]{1,0:T(8,128)(2,1)}, u32[]{:S(2)}, u32[]{:S(2)}) %collective-permute-start.73) | collective-permute-done | bytes 614432 | tf_op jit(solution)/shard_map/ppermute | solution.py:133
  648.6 21.9 %collective-permute-done.75 = bf16[1,400,768]{2,1,0:T(8,128)(2,1)S(1)} collective-permute-done((bf16[1,400,768]{2,1,0:T(8,128)(2,1)S(1)}, bf16[1,400,768]{2,1,0:T(8,128)(2,1)S(1)}, u32[]{:S(2)}, u32[]{:S(2)}) %collective-permute-start.75) | collective-permute-done | bytes 614432 | tf_op jit(solution)/shard_map/ppermute | solution.py:53
  719.2 11.5 %collective-permute-done.81 = bf16[224,1600]{1,0:T(8,128)(2,1)S(1)} collective-permute-done((bf16[224,1600]{1,0:T(8,128)(2,1)S(1)}, bf16[224,1600]{1,0:T(8,128)(2,1)S(1)}, u32[]{:S(2)}, u32[]{:S(2)}) %collective-permute-start.81) | collective-permute-done | bytes 716832 | tf_op jit(solution)/shard_map/ppermute | solution.py:56
  730.8 14.5 %collective-permute-done.80 = bf16[224,1600]{1,0:T(8,128)(2,1)S(1)} collective-permute-done((bf16[224,1600]{1,0:T(8,128)(2,1)S(1)}, bf16[224,1600]{1,0:T(8,128)(2,1)S(1)}, u32[]{:S(2)}, u32[]{:S(2)}) %collective-permute-start.80) | collective-permute-done | bytes 716832 | tf_op jit(solution)/shard_map/ppermute | solution.py:56
  751.6 10.6 %concatenate.162 = bf16[400,6400]{1,0:T(8,128)(2,1)} concatenate(bf16[400,800]{1,0:T(8,128)(2,1)} %get-tuple-element.98, bf16[400,800]{1,0:T(8,128)(2,1)} %get-tuple-element.97, bf16[400,800]{1,0:T(8,128)(2,1)} %get-tuple-element.96, bf16[400,800]{1,0:T(8,128)(2,1)} %get-tuple-element.95, bf16[400,800]{1,0:T(8,128)(2,1)} %get-tuple-element.94, ...), dimensions={1} | concatenate | bytes 10240000 | tf_op jit(solution)/shard_map/concatenate | solution.py:418
  793.3 10.1 %concatenate.165 = bf16[6400,400]{0,1:T(8,128)(2,1)} concatenate(bf16[800,400]{0,1:T(8,128)(2,1)} %get-tuple-element.87, bf16[800,400]{0,1:T(8,128)(2,1)} %get-tuple-element.86, bf16[800,400]{0,1:T(8,128)(2,1)} %get-tuple-element.85, bf16[800,400]{0,1:T(8,128)(2,1)} %get-tuple-element.84, bf16[800,400]{0,1:T(8,128)(2,1)} %get-tuple-element.83, ...), dimensions={0} | concatenate | bytes 10240000 | tf_op jit(solution)/shard_map/concatenate | solution.py:416
  (545 shorter events, 484.9 us)
Async XLA Ops:
  6.3 45.5 %collective-permute-start = (bf16[12,400]{1,0:T(8,128)(2,1)S(1)}, bf16[12,400]{1,0:T(8,128)(2,1)S(1)}, u32[]{:S(2)}, u32[]{:S(2)}) collective-permute-start(bf16[12,400]{1,0:T(8,128)(2,1)S(1)} %concatenate.132), channel_id=1, source_target_pairs={{0,1},{1,2},{2,3},{4,5},{5,6},{6,7},{8,9},{9,10},{10,11},{12,13},{... | collective-permute-start | bytes 28808 | tf_op jit(solution)/shard_map/ppermute | solution.py:104
  17.2 44.8 %collective-permute-start.19 = (bf16[56,1600]{1,0:T(8,128)(2,1)S(1)}, bf16[56,1600]{1,0:T(8,128)(2,1)}, u32[]{:S(2)}, u32[]{:S(2)}) collective-permute-start(bf16[56,1600]{1,0:T(8,128)(2,1)S(1)} %pad_dynamic-slice_fusion.3), channel_id=1, source_target_pairs={{0,1},{1,2},{2,3},{4,5},{5,6},{6,7},{8,9},{9,10},{10,11},{12,13},{... | collective-permute-start | bytes 537608 | tf_op jit(solution)/shard_map/ppermute | solution.py:104
  54.9 54.7 %collective-permute-start.8 = (bf16[400,768]{1,0:T(8,128)(2,1)}, bf16[400,768]{1,0:T(8,128)(2,1)}, u32[]{:S(2)}, u32[]{:S(2)}) collective-permute-start(bf16[400,768]{1,0:T(8,128)(2,1)} %pad_maximum_fusion.10), channel_id=1, source_target_pairs={{0,1},{1,2},{2,3},{4,5},{5,6},{6,7},{8,9},{9,10},{10,11},{12,13},{... | collective-permute-start | bytes 1843208 | tf_op jit(solution)/shard_map/ppermute | solution.py:104
  57.8 54.1 %collective-permute-start.9 = (bf16[400,768]{1,0:T(8,128)(2,1)}, bf16[400,768]{1,0:T(8,128)(2,1)}, u32[]{:S(2)}, u32[]{:S(2)}) collective-permute-start(bf16[400,768]{1,0:T(8,128)(2,1)} %pad_maximum_fusion.10), channel_id=1, source_target_pairs={{1,0},{2,1},{3,2},{5,4},{6,5},{7,6},{9,8},{10,9},{11,10},{13,12},{... | collective-permute-start | bytes 1843208 | tf_op jit(solution)/shard_map/ppermute | solution.py:105
  111.9 58.8 %collective-permute-start.7 = (bf16[512,1600]{0,1:T(8,128)(2,1)S(1)}, bf16[512,1600]{0,1:T(8,128)(2,1)S(1)}, u32[]{:S(2)}, u32[]{:S(2)}) collective-permute-start(bf16[512,1600]{0,1:T(8,128)(2,1)S(1)} %pad_maximum_fusion.6), channel_id=1, source_target_pairs={{0,4},{4,0},{8,12},{12,8},{16,20},{20,16},{24,28},{28,24},{1,5},{5... | collective-permute-start | bytes 4915208 | tf_op jit(solution)/shard_map/ppermute | solution.py:56
  126.7 120.8 %collective-permute-start.32 = (bf16[400,800]{1,0:T(8,128)(2,1)}, bf16[400,800]{1,0:T(8,128)(2,1)}, u32[]{:S(2)}, u32[]{:S(2)}) collective-permute-start(bf16[400,800]{1,0:T(8,128)(2,1)} %constant_dynamic-slice_fusion.5), channel_id=1, source_target_pairs={{1,0},{2,1},{3,2},{5,4},{6,5},{7,6},{9,8},{10,9},{11,10},{13,12},{... | collective-permute-start | bytes 1920008 | tf_op jit(solution)/shard_map/ppermute | solution.py:105
  128.4 119.7 %collective-permute-start.33 = (bf16[400,800]{1,0:T(8,128)(2,1)}, bf16[400,800]{1,0:T(8,128)(2,1)}, u32[]{:S(2)}, u32[]{:S(2)}) collective-permute-start(bf16[400,800]{1,0:T(8,128)(2,1)} %constant_dynamic-slice_fusion.5), channel_id=1, source_target_pairs={{0,2},{1,3},{2,0},{3,1},{4,6},{5,7},{6,4},{7,5},{8,10},{9,11},{10,... | collective-permute-start | bytes 1920008 | tf_op jit(solution)/shard_map/ppermute | solution.py:106
  144.7 104.4 %collective-permute-start.35 = (bf16[400,800]{1,0:T(8,128)(2,1)}, bf16[400,800]{1,0:T(8,128)(2,1)}, u32[]{:S(2)}, u32[]{:S(2)}) collective-permute-start(bf16[400,800]{1,0:T(8,128)(2,1)} %dynamic-slice_bitcast_fusion.20), channel_id=1, source_target_pairs={{0,1},{1,2},{2,3},{4,5},{5,6},{6,7},{8,9},{9,10},{10,11},{12,13},{... | collective-permute-start | bytes 1920008 | tf_op jit(solution)/shard_map/ppermute | solution.py:104
  170.6 58.6 %collective-permute-start.26 = (bf16[4,224,1600]{2,1,0:T(8,128)(2,1)}, bf16[4,224,1600]{2,1,0:T(8,128)(2,1)}, u32[]{:S(2)}, u32[]{:S(2)}) collective-permute-start(bf16[4,224,1600]{2,1,0:T(8,128)(2,1)} %pad_maximum_fusion.1), channel_id=1, source_target_pairs={{0,4},{4,0},{8,12},{12,8},{16,20},{20,16},{24,28},{28,24},{1,5},{5... | collective-permute-start | bytes 8601608 | tf_op jit(solution)/shard_map/ppermute | solution.py:56
  247.6 60.0 %collective-permute-start.46 = (bf16[512,1600]{0,1:T(8,128)(2,1)S(1)}, bf16[512,1600]{0,1:T(8,128)(2,1)S(1)}, u32[]{:S(2)}, u32[]{:S(2)}) collective-permute-start(bf16[512,1600]{0,1:T(8,128)(2,1)S(1)} %copy-done.27), channel_id=1, source_target_pairs={{0,4},{4,0},{8,12},{12,8},{16,20},{20,16},{24,28},{28,24},{1,5},{5... | collective-permute-start | bytes 4915208 | tf_op jit(solution)/shard_map/ppermute | solution.py:56
  327.7 115.9 %collective-permute-start.47 = (bf16[512,1600]{0,1:T(8,128)(2,1)}, bf16[512,1600]{0,1:T(8,128)(2,1)}, u32[]{:S(2)}, u32[]{:S(2)}) collective-permute-start(bf16[512,1600]{0,1:T(8,128)(2,1)} %convolution_convert_fusion), channel_id=1, source_target_pairs={{0,4},{4,0},{8,12},{12,8},{16,20},{20,16},{24,28},{28,24},{1,5},{5... | collective-permute-start | bytes 4915208 | tf_op jit(solution)/shard_map/ppermute | solution.py:56
  329.5 48.1 %collective-permute-start.91 = (bf16[400,800]{1,0:T(8,128)(2,1)S(1)}, bf16[400,800]{1,0:T(8,128)(2,1)S(1)}, u32[]{:S(2)}, u32[]{:S(2)}) collective-permute-start(bf16[400,800]{1,0:T(8,128)(2,1)S(1)} %get-tuple-element.101), channel_id=1, source_target_pairs={{1,0},{2,1},{3,2},{5,4},{6,5},{7,6},{9,8},{10,9},{11,10},{13,12},{... | collective-permute-start | bytes 1920008 | tf_op jit(solution)/shard_map/ppermute | solution.py:131
  330.8 48.1 %collective-permute-start.90 = (bf16[400,800]{1,0:T(8,128)(2,1)S(1)}, bf16[400,800]{1,0:T(8,128)(2,1)S(1)}, u32[]{:S(2)}, u32[]{:S(2)}) collective-permute-start(bf16[400,800]{1,0:T(8,128)(2,1)S(1)} %get-tuple-element.99), channel_id=1, source_target_pairs={{0,1},{1,2},{2,3},{4,5},{5,6},{6,7},{8,9},{9,10},{10,11},{12,13},{... | collective-permute-start | bytes 1920008 | tf_op jit(solution)/shard_map/ppermute | solution.py:130
  345.9 46.0 %collective-permute-start.93 = (bf16[400,800]{1,0:T(8,128)(2,1)S(1)}, bf16[400,800]{1,0:T(8,128)(2,1)S(1)}, u32[]{:S(2)}, u32[]{:S(2)}) collective-permute-start(bf16[400,800]{1,0:T(8,128)(2,1)S(1)} %fusion.14), channel_id=1, source_target_pairs={{0,2},{1,3},{2,0},{3,1},{4,6},{5,7},{6,4},{7,5},{8,10},{9,11},{10,... | collective-permute-start | bytes 1920008 | tf_op jit(solution)/shard_map/ppermute | solution.py:133
  376.5 71.4 %collective-permute-start.39 = (bf16[512,1600]{0,1:T(8,128)(2,1)}, bf16[512,1600]{0,1:T(8,128)(2,1)}, u32[]{:S(2)}, u32[]{:S(2)}) collective-permute-start(bf16[512,1600]{0,1:T(8,128)(2,1)} %convolution_convert_fusion.1), channel_id=1, source_target_pairs={{0,4},{4,0},{8,12},{12,8},{16,20},{20,16},{24,28},{28,24},{1,5},{5... | collective-permute-start | bytes 4915208 | tf_op jit(solution)/shard_map/ppermute | solution.py:56
  392.8 47.1 %collective-permute-start.101 = (bf16[400,800]{1,0:T(8,128)(2,1)}, bf16[400,800]{1,0:T(8,128)(2,1)}, u32[]{:S(2)}, u32[]{:S(2)}) collective-permute-start(bf16[400,800]{1,0:T(8,128)(2,1)} %fusion.10), channel_id=1, source_target_pairs={{0,2},{1,3},{2,0},{3,1},{4,6},{5,7},{6,4},{7,5},{8,10},{9,11},{10,... | collective-permute-start | bytes 1920008 | tf_op jit(solution)/shard_map/ppermute | solution.py:133
  399.0 54.1 %collective-permute-start.94 = (bf16[1,400,800]{2,1,0:T(8,128)(2,1)S(1)}, bf16[1,400,800]{2,1,0:T(8,128)(2,1)S(1)}, u32[]{:S(2)}, u32[]{:S(2)}) collective-permute-start(bf16[1,400,800]{2,1,0:T(8,128)(2,1)S(1)} %get-tuple-element.45), channel_id=1, source_target_pairs={{0,8},{4,12},{8,0},{12,4},{16,24},{20,28},{24,16},{28,20},{1,9},{5... | collective-permute-start | bytes 1920008 | tf_op jit(solution)/shard_map/ppermute | solution.py:53
  407.3 47.3 %collective-permute-start.95 = (bf16[1,400,800]{2,1,0:T(8,128)(2,1)S(1)}, bf16[1,400,800]{2,1,0:T(8,128)(2,1)S(1)}, u32[]{:S(2)}, u32[]{:S(2)}) collective-permute-start(bf16[1,400,800]{2,1,0:T(8,128)(2,1)S(1)} %get-tuple-element.45), channel_id=1, source_target_pairs={{0,16},{4,20},{8,24},{12,28},{16,0},{20,4},{24,8},{28,12},{1,17},{... | collective-permute-start | bytes 1920008 | tf_op jit(solution)/shard_map/ppermute | solution.py:53
  454.5 44.7 %collective-permute-start.50 = (bf16[128,1600]{0,1:T(8,128)(2,1)S(1)}, bf16[128,1600]{0,1:T(8,128)(2,1)S(1)}, u32[]{:S(2)}, u32[]{:S(2)}) collective-permute-start(bf16[128,1600]{0,1:T(8,128)(2,1)S(1)} %get-tuple-element.125), channel_id=1, source_target_pairs={{0,24},{4,28},{8,16},{12,20},{16,8},{20,12},{24,0},{28,4},{1,25},{... | collective-permute-start | bytes 1228808 | tf_op jit(solution)/shard_map/ppermute | solution.py:56
  459.7 48.3 %collective-permute-start.49 = (bf16[128,1600]{0,1:T(8,128)(2,1)S(1)}, bf16[128,1600]{0,1:T(8,128)(2,1)S(1)}, u32[]{:S(2)}, u32[]{:S(2)}) collective-permute-start(bf16[128,1600]{0,1:T(8,128)(2,1)S(1)} %get-tuple-element.126), channel_id=1, source_target_pairs={{0,16},{4,20},{8,24},{12,28},{16,0},{20,4},{24,8},{28,12},{1,17},{... | collective-permute-start | bytes 1228808 | tf_op jit(solution)/shard_map/ppermute | solution.py:56
  582.1 52.4 %collective-permute-start.58 = (bf16[512,1600]{0,1:T(8,128)(2,1)}, bf16[512,1600]{0,1:T(8,128)(2,1)}, u32[]{:S(2)}, u32[]{:S(2)}) collective-permute-start(bf16[512,1600]{0,1:T(8,128)(2,1)} %convolution_convert_fusion.2), channel_id=1, source_target_pairs={{0,4},{4,0},{8,12},{12,8},{16,20},{20,16},{24,28},{28,24},{1,5},{5... | collective-permute-start | bytes 4915208 | tf_op jit(solution)/shard_map/ppermute | solution.py:56
  670.5 45.1 %collective-permute-start.97 = (bf16[4,400,800]{2,1,0:T(8,128)(2,1)}, bf16[4,400,800]{2,1,0:T(8,128)(2,1)}, u32[]{:S(2)}, u32[]{:S(2)}) collective-permute-start(bf16[4,400,800]{2,1,0:T(8,128)(2,1)} %pad_maximum_fusion.3), channel_id=1, source_target_pairs={{0,4},{4,0},{8,12},{12,8},{16,20},{20,16},{24,28},{28,24},{1,5},{5... | collective-permute-start | bytes 7680008 | tf_op jit(solution)/shard_map/ppermute | solution.py:56
  670.6 107.5 %collective-permute-start.105 = (bf16[4,800,400]{1,2,0:T(8,128)(2,1)}, bf16[4,800,400]{1,2,0:T(8,128)(2,1)}, u32[]{:S(2)}, u32[]{:S(2)}) collective-permute-start(bf16[4,800,400]{1,2,0:T(8,128)(2,1)} %pad_maximum_fusion.4), channel_id=1, source_target_pairs={{0,4},{4,0},{8,12},{12,8},{16,20},{20,16},{24,28},{28,24},{1,5},{5... | collective-permute-start | bytes 7680008 | tf_op jit(solution)/shard_map/ppermute | solution.py:56
  715.6 102.6 %collective-permute-start.77 = (bf16[4,400,768]{2,1,0:T(8,128)(2,1)}, bf16[4,400,768]{2,1,0:T(8,128)(2,1)}, u32[]{:S(2)}, u32[]{:S(2)}) collective-permute-start(bf16[4,400,768]{2,1,0:T(8,128)(2,1)} %pad_maximum_fusion.5), channel_id=1, source_target_pairs={{0,4},{4,0},{8,12},{12,8},{16,20},{20,16},{24,28},{28,24},{1,5},{5... | collective-permute-start | bytes 7372808 | tf_op jit(solution)/shard_map/ppermute | solution.py:56
  (128 other events, 2475.7 us)

commit v2 on v1

v2 whole, which is shorter than its diff:
```python
import math

import jax
import jax.numpy as jnp
from jax import lax
from jax.experimental import pallas as pl
from jax.experimental.pallas import tpu as pltpu
from jax.sharding import PartitionSpec as P

H = 25
HD = 64
ROWS = 256

f32 = jnp.float32
bf16 = jnp.bfloat16

VMEM = pl.BlockSpec(memory_space=pltpu.VMEM)
SMEM = pl.BlockSpec(memory_space=pltpu.SMEM)
ANY = pl.BlockSpec(memory_space=pl.ANY)


def shape(*dims, dtype=bf16):
    return jax.ShapeDtypeStruct(dims, dtype)


def matmul(left, right, left_dim, right_dim):
    return lax.dot_general(
        left, right, (((left_dim,), (right_dim,)), ((), ())), preferred_element_type=f32
    )


def norm_parts(values):
    centre = jnp.mean(values, axis=-1, keepdims=True)
    shifted = values - centre
    spread = jnp.mean(shifted * shifted, axis=-1, keepdims=True)
    inverse = lax.rsqrt(spread + 1e-05)
    return shifted * inverse, inverse


def norm_back(cot, values, gain):
    normal, inverse = norm_parts(values)
    scaled = cot * gain
    first = jnp.mean(scaled, axis=-1, keepdims=True)
    second = jnp.mean(scaled * normal, axis=-1, keepdims=True)
    back = inverse * (scaled - first - normal * second)
    return (
        back,
        jnp.sum(cot * normal, axis=0, keepdims=True),
        jnp.sum(cot, axis=0, keepdims=True),
    )


class Plane:
    def __init__(self, size):
        self.size = size
        self.chips = size // 2
        self.wide = math.isqrt(self.chips)
        self.tall = self.chips // self.wide
        self.shifts = [(da, db) for da in range(self.tall) for db in range(self.wide)]
        self.me = lax.axis_index("ctx")
        places = [self.index_of(slot) for slot in range(size)]
        self.places = jnp.stack(places).astype(jnp.int32)

    def _moved(self, chip, shift, sign):
        row, col = chip // self.wide, chip % self.wide
        row = (row + sign * shift[0] + self.tall) % self.tall
        col = (col + sign * shift[1] + self.wide) % self.wide
        return row * self.wide + col

    def index_of(self, slot):
        core = self.me % 2
        if slot >= self.chips:
            core = 1 - core
        return self._moved(self.me // 2, self.shifts[slot % self.chips], -1) * 2 + core

    def _pairs(self, slot, sign):
        shift, flip = self.shifts[slot % self.chips], slot // self.chips
        return [
            (i, self._moved(i // 2, shift, sign) * 2 + (i % 2 + flip) % 2)
            for i in range(self.size)
        ]

    def from_slot(self, value, slot):
        return lax.ppermute(value, "ctx", self._pairs(slot, 1))

    def to_slot(self, value, slot):
        return lax.ppermute(value, "ctx", self._pairs(slot, -1))

    def opposite(self, slot):
        da, db = self.shifts[slot % self.chips]
        shift = ((self.tall - da) % self.tall, (self.wide - db) % self.wide)
        return self.shifts.index(shift) + self.chips * (slot // self.chips)

    def swap(self, value):
        return self.to_slot(value, self.chips)

    def gather(self, value):
        mine = [value] + [self.from_slot(value, slot) for slot in range(1, self.chips)]
        return mine + [self.swap(piece) for piece in mine]

    def exchange(self, pieces):
        got = [pieces[0]] + [None] * (self.size - 1)
        for slot in range(1, self.size):
            got[self.opposite(slot)] = self.to_slot(pieces[slot], slot)
        return got

    def scatter(self, mine, theirs):
        received = self.swap(theirs)
        chips, dims = self.chips, mine.shape[1:]

        def kernel(places, mine_ref, received_ref, own_ref, *sent):
            def total(slot):
                chip = places[slot] // 2
                return mine_ref[chip].astype(f32) + received_ref[chip].astype(f32)

            own_ref[...] = total(0)
            for slot in range(1, chips):
                sent[slot - 1][...] = total(slot).astype(bf16)

        own, *sent = pl.pallas_call(
            kernel,
            out_shape=[shape(*dims, dtype=f32)] + [shape(*dims)] * (chips - 1),
            in_specs=[SMEM, VMEM, VMEM],
            out_specs=[VMEM] * chips,
            name="pair_sum",
        )(self.places, mine, received)
        return [own] + [self.to_slot(sent[slot - 1], slot) for slot in range(1, chips)]

    def collect(self, pieces):
        dims = pieces[0].shape
        count = len(pieces)

        def kernel(places, *refs):
            parts, out, sems = refs[:count], refs[count], refs[count + 1]
            copies = [
                pltpu.make_async_copy(parts[i], out.at[places[i]], sems.at[i])
                for i in range(count)
            ]
            for copy in copies:
                copy.start()
            for copy in copies:
                copy.wait()

        return pl.pallas_call(
            kernel,
            out_shape=shape(count, *dims, dtype=pieces[0].dtype),
            in_specs=[SMEM] + [ANY] * count,
            out_specs=ANY,
            scratch_shapes=[pltpu.SemaphoreType.DMA((count,))],
            name="collect",
        )(self.places, *pieces)


def line_gather(value, size):
    at = lax.axis_index("fsdp")
    if size != 4:
        return lax.all_gather(value, "fsdp", axis=0, tiled=True)
    up = lax.ppermute(value, "fsdp", [(0, 1), (1, 2), (2, 3)])
    down = lax.ppermute(value, "fsdp", [(1, 0), (2, 1), (3, 2)])
    cross = lax.ppermute(value, "fsdp", [(0, 2), (1, 3), (2, 0), (3, 1)])
    relay = lax.ppermute(cross, "fsdp", [(2, 3), (1, 0)])
    rows = value.shape[0]

    def kernel(at_ref, own_ref, up_ref, down_ref, cross_ref, relay_ref, out_ref, sems):
        here = at_ref[0]

        def copy(ref, block, sem):
            to = pl.ds(pl.multiple_of(block * rows, rows), rows)
            return pltpu.make_async_copy(ref, out_ref.at[to], sems.at[sem])

        steps = [
            (None, copy(own_ref, here, 0)),
            (None, copy(cross_ref, (here + 2) % 4, 1)),
            (here == 0, copy(relay_ref, 3, 2)),
            (here != 0, copy(up_ref, (here + 3) % 4, 2)),
            (here == 3, copy(relay_ref, 0, 3)),
            (here != 3, copy(down_ref, (here + 1) % 4, 3)),
        ]
        for act in (lambda c: c.start(), lambda c: c.wait()):
            for when, step in steps:
                if when is None:
                    act(step)
                else:
                    pl.when(when)(lambda step=step, act=act: act(step))

    return pl.pallas_call(
        kernel,
        out_shape=shape(size * rows, value.shape[1]),
        in_specs=[SMEM] + [ANY] * 5,
        out_specs=ANY,
        scratch_shapes=[pltpu.SemaphoreType.DMA((4,))],
        name="line_collect",
    )(at.astype(jnp.int32)[None], value, up, down, cross, relay)


def line_scatter(parts):
    return lax.psum_scatter(parts, "fsdp", scatter_dimension=0, tiled=False)


def _blocks(length):
    count = length // ROWS
    return count, count <= 4


def _scores(key_head, query_block, first):
    scores = matmul(key_head, query_block, 1, 1)
    key_at = lax.broadcasted_iota(jnp.int32, scores.shape, 0)
    query_at = lax.broadcasted_iota(jnp.int32, scores.shape, 1) + first
    return scores, key_at <= query_at


def _sweep(length, block):
    count, few = _blocks(length)
    if few:
        for index in range(count):
            block(index, (index + 1) * ROWS)
    else:
        lax.fori_loop(0, count, lambda i, c: (block(i, length), c)[1], 0)


def attend(heads, plane, query, key, value):
    length, width = query.shape
    slots = plane.size
    rows = length // slots

    def kernel(places, q_ref, k_ref, v_ref, *refs):
        outs, (out_t_ref, log_ref, o_s) = refs[:slots], refs[slots:]
        for head in range(heads):
            cols = slice(head * HD, (head + 1) * HD)

            def block(index, until, head=head, cols=cols):
                at = pl.ds(index * ROWS, ROWS)
                scores, kept = _scores(k_ref[0:until, cols], q_ref[at, cols], index * ROWS)
                scores = jnp.where(kept, scores, -1e30)
                top = jnp.max(scores, axis=0, keepdims=True)
                weights = jnp.exp(scores - top)
                total = jnp.sum(weights, axis=0, keepdims=True)
                summed = matmul(v_ref[0:until, cols].T, weights.astype(bf16), 1, 0)
                out_t_ref[cols, at] = summed / total
                log_ref[head : head + 1, at] = top + jnp.log(total)

            _sweep(length, block)
        o_s[...] = out_t_ref[...].T.astype(bf16)
        for slot in range(slots):
            outs[slot][...] = o_s[pl.ds(pl.multiple_of(places[slot] * rows, rows), rows), :]

    *pieces, out_t, log_total = pl.pallas_call(
        kernel,
        out_shape=[shape(rows, width)] * slots
        + [shape(width, length, dtype=f32), shape(heads, length, dtype=f32)],
        in_specs=[SMEM, VMEM, VMEM, VMEM],
        out_specs=[VMEM] * (slots + 2),
        scratch_shapes=[pltpu.VMEM((length, width), bf16)],
        name="attend",
    )(plane.places, query, key, value)
    return pieces, out_t, log_total


def attend_back(heads, plane, query, key, value, cots, out_t, log_total):
    length, width = query.shape
    slots = plane.size
    rows = length // slots

    def kernel(places, q_ref, k_ref, v_ref, out_t_ref, log_ref, *refs):
        cot_refs, (g_ref, d_s, dk_s, dv_s, dq_t) = refs[:slots], refs[slots:]
        for slot in range(slots):
            d_s[pl.ds(pl.multiple_of(places[slot] * rows, rows), rows), :] = cot_refs[slot][...]
        dk_s[...] = jnp.zeros_like(dk_s)
        dv_s[...] = jnp.zeros_like(dv_s)
        for head in range(heads):
            cols = slice(head * HD, (head + 1) * HD)

            def block(index, until, head=head, cols=cols):
                at = pl.ds(index * ROWS, ROWS)
                query, cot = q_ref[at, cols], d_s[at, cols]
                delta = jnp.sum(cot.astype(f32).T * out_t_ref[cols, at], axis=0, keepdims=True)
                scores, kept = _scores(k_ref[0:until, cols], query, index * ROWS)
                weights = jnp.where(kept, jnp.exp(scores - log_ref[head : head + 1, at]), 0.0)
                d_weights = matmul(v_ref[0:until, cols], cot, 1, 1)
                d_scores = (weights * (d_weights - delta)).astype(bf16)
                dv_s[head, 0:until, :] += matmul(weights.astype(bf16), cot, 1, 0)
                dk_s[head, 0:until, :] += matmul(d_scores, query, 1, 0)
                dq_t[cols, at] = matmul(k_ref[0:until, cols].T, d_scores, 1, 0)

            _sweep(length, block)
        scale = 1.0 / math.sqrt(HD)
        g_ref[:, 0:width] = (dq_t[...] * scale).T.astype(bf16)
        for head in range(heads):
            at = width + head * HD
            g_ref[:, at : at + HD] = dk_s[head].astype(bf16)
            g_ref[:, at + width : at + width + HD] = dv_s[head].astype(bf16)

    return pl.pallas_call(
        kernel,
        out_shape=shape(length, 3 * width),
        in_specs=[SMEM] + [VMEM] * (5 + slots),
        out_specs=VMEM,
        scratch_shapes=[pltpu.VMEM((length, width), bf16)]
        + [pltpu.VMEM((heads, length, HD), f32)] * 2
        + [pltpu.VMEM((width, length), f32)],
        name="attend_back",
    )(plane.places, query, key, value, out_t, log_total, *cots)


def rows_spec(rows, width):
    return pl.BlockSpec((rows, width), lambda i: (i, 0))


def whole_spec(dims):
    return pl.BlockSpec(dims, lambda i: (0,) * len(dims), pipeline_mode=pl.Buffered(1))


def chip_spec(rows, width):
    return pl.BlockSpec((1, rows, width), lambda i: (i, 0, 0))


def project(plane, tokens, weight, gain, bias, bias_q, bias_v, span):
    length, width = tokens.shape
    rows = length // plane.chips

    def kernel(x_ref, w_ref, gain_ref, bias_ref, bq_ref, bv_ref, n_ref, q_ref, k_ref, v_ref):
        normal, _ = norm_parts(x_ref[...].astype(f32))
        normed = (normal * gain_ref[...] + bias_ref[...]).astype(bf16)
        n_ref[...] = normed
        made = matmul(normed, w_ref[:, 0 : 3 * span], 1, 0)
        queries = (made[:, 0:span] + bq_ref[...]).astype(bf16)
        q_ref[...] = queries * jnp.asarray(1.0 / math.sqrt(HD), bf16)
        k_ref[...] = made[:, span : 2 * span].astype(bf16)
        v_ref[...] = (made[:, 2 * span : 3 * span] + bv_ref[...]).astype(bf16)

    return pl.pallas_call(
        kernel,
        grid=(plane.chips,),
        out_shape=[shape(length, width)] + [shape(length, span)] * 3,
        in_specs=[rows_spec(rows, width)]
        + [whole_spec(v.shape) for v in (weight, gain, bias, bias_q, bias_v)],
        out_specs=[rows_spec(rows, width)] + [rows_spec(rows, span)] * 3,
        name="project",
    )(tokens, weight, gain, bias, bias_q, bias_v)


def split_store(core, part, scratch, mine_ref, theirs_ref):
    rows = scratch.shape[0] // 2
    scratch[...] = part.astype(bf16)
    mine_ref[0] = scratch[pl.ds(pl.multiple_of(core * rows, rows), rows), :]
    theirs_ref[0] = scratch[pl.ds(pl.multiple_of((1 - core) * rows, rows), rows), :]


def partial_rows(plane, left, weight, first, count, name):
    length = left.shape[0]
    width = weight.shape[0]
    rows = length // plane.chips

    def kernel(core, left_ref, w_ref, mine_ref, theirs_ref, scratch):
        part = matmul(left_ref[...], w_ref[:, first : first + count], 1, 1)
        split_store(core[0], part, scratch, mine_ref, theirs_ref)

    return pl.pallas_call(
        kernel,
        grid=(plane.chips,),
        out_shape=[shape(plane.chips, rows // 2, width)] * 2,
        in_specs=[SMEM, rows_spec(rows, count), whole_spec(weight.shape)],
        out_specs=[chip_spec(rows // 2, width)] * 2,
        scratch_shapes=[pltpu.VMEM((rows, width), bf16)],
        name=name,
    )(plane.me.astype(jnp.int32)[None] % 2, left, weight)


def feed_forward(plane, normed, cots, weight, bias):
    length, width = normed.shape
    rows = length // plane.chips
    part = weight.shape[1] // 2

    def kernel(core, n_ref, c_ref, w_ref, b_ref, a_ref, d_ref, sum_ref, mine_ref, theirs_ref, scratch):
        pre = matmul(n_ref[...], w_ref[:, 0:part], 1, 0) + b_ref[...]
        back = matmul(c_ref[...], w_ref[:, part : 2 * part], 1, 0)
        root = math.sqrt(2.0 / math.pi)
        square = pre * pre
        bend = jnp.tanh(root * (pre + 0.044715 * (pre * square)))
        half = 0.5 * (1.0 + bend)
        a_ref[...] = (pre * half).astype(bf16)
        slope = half + 0.5 * pre * (1.0 - bend * bend) * (root * (1.0 + 3 * 0.044715 * square))
        d_pre = (back * slope).astype(bf16)
        d_ref[...] = d_pre

        @pl.when(pl.program_id(0) == 0)
        def _():
            sum_ref[...] = jnp.zeros_like(sum_ref)

        sum_ref[...] += jnp.sum(d_pre.astype(f32), axis=0, keepdims=True)
        given = matmul(d_pre, w_ref[:, 0:part], 1, 1)
        split_store(core[0], given, scratch, mine_ref, theirs_ref)

    return pl.pallas_call(
        kernel,
        grid=(plane.chips,),
        out_shape=[shape(length, part)] * 2
        + [shape(1, part, dtype=f32)]
        + [shape(plane.chips, rows // 2, width)] * 2,
        in_specs=[SMEM, rows_spec(rows, width), rows_spec(rows, width)]
        + [whole_spec(weight.shape), whole_spec(bias.shape)],
        out_specs=[rows_spec(rows, part)] * 2
        + [pl.BlockSpec((1, part), lambda i: (0, 0))]
        + [chip_spec(rows // 2, width)] * 2,
        scratch_shapes=[pltpu.VMEM((rows, width), bf16)],
        name="feed_forward",
    )(plane.me.astype(jnp.int32)[None] % 2, normed, cots, weight, bias)


def branch_norm(plane, pieces, weights, tokens, bias, gain, bias_two):
    rows, width = tokens.shape
    slots = plane.size
    span = pieces[0].shape[1]
    part = weights.shape[2]

    def kernel(places, w_ref, x_ref, bias_ref, gain_ref, bias_two_ref, *refs):
        parts, (resid_ref, normed_ref, out_ref, o_s) = refs[:slots], refs[slots:]
        for slot in range(slots):
            o_s[places[slot]] = parts[slot][...]
        for j in range(slots):
            until = min((j + 1) * span, width)
            if j * span < width:
                out_ref[:, j * span : until] = o_s[j][:, 0 : until - j * span]
        out = out_ref[...]
        for j in range(slots):
            at = slice(j * part, (j + 1) * part)
            made = matmul(out, w_ref[j], 1, 0)
            resid_ref[:, at] = x_ref[:, at].astype(f32) + made + bias_ref[:, at]
        normal, _ = norm_parts(resid_ref[...])
        normed_ref[...] = (normal * gain_ref[...] + bias_two_ref[...]).astype(bf16)

    return pl.pallas_call(
        kernel,
        out_shape=[shape(rows, width, dtype=f32), shape(rows, width), shape(rows, width)],
        in_specs=[SMEM] + [VMEM] * (5 + slots),
        out_specs=[VMEM] * 3,
        scratch_shapes=[pltpu.VMEM((slots, rows, span), bf16)],
        name="branch_norm",
    )(plane.places, weights, tokens, bias, gain, bias_two, *pieces)


def branch_back(plane, terms, resid, cot, gain, weights, span):
    rows, width = resid.shape
    slots = plane.size
    part = weights.shape[2]
    count = len(terms)

    def kernel(places, resid_ref, cot_ref, gain_ref, w_ref, *refs):
        term_refs, refs = refs[:count], refs[count:]
        d_resid_ref, d_branch_ref, d_gain_ref, d_bias_ref = refs[:4]
        outs, d_s, padded = refs[4 : 4 + slots], refs[4 + slots], refs[5 + slots]
        total = term_refs[0][...]
        for term in term_refs[1:]:
            total = total + term[...].astype(f32)
        back, d_gain_ref[...], d_bias_ref[...] = norm_back(total, resid_ref[...], gain_ref[...])
        d_resid = cot_ref[...].astype(f32) + back
        d_resid_ref[...] = d_resid
        d_branch_ref[...] = d_resid.astype(bf16)
        given = jnp.zeros((rows, width), f32)
        for j in range(slots):
            at = slice(j * part, (j + 1) * part)
            given = given + matmul(d_branch_ref[:, at], w_ref[j], 1, 1)
        padded[...] = jnp.zeros_like(padded)
        padded[:, 0:width] = given.astype(bf16)
        for j in range(slots):
            d_s[j] = padded[:, j * span : (j + 1) * span]
        for slot in range(slots):
            outs[slot][...] = d_s[places[slot]]

    d_resid, d_branch, d_gain, d_bias, *pieces = pl.pallas_call(
        kernel,
        out_shape=[shape(rows, width, dtype=f32), shape(rows, width)]
        + [shape(1, width, dtype=f32)] * 2
        + [shape(rows, span)] * slots,
        in_specs=[SMEM] + [VMEM] * (4 + count),
        out_specs=[VMEM] * (4 + slots),
        scratch_shapes=[
            pltpu.VMEM((slots, rows, span), bf16),
            pltpu.VMEM((rows, slots * span), bf16),
        ],
        name="branch_back",
    )(plane.places, resid, cot, gain, weights, *terms)
    return d_resid, d_branch, d_gain, d_bias, pieces


def out_weight_parts(plane, left, right, part):
    rows, width = left.shape

    def kernel(core, left_ref, right_ref, mine_ref, theirs_ref, left_t, r_s):
        @pl.when(pl.program_id(0) == 0)
        def _():
            left_t[...] = left_ref[...].T
            for j in range(plane.size):
                r_s[j] = right_ref[:, j * part : (j + 1) * part]

        at = pl.program_id(0) * 2
        mine_ref[0] = matmul(left_t[...], r_s[at + core[0]], 1, 0).astype(bf16)
        theirs_ref[0] = matmul(left_t[...], r_s[at + 1 - core[0]], 1, 0).astype(bf16)

    return pl.pallas_call(
        kernel,
        grid=(plane.chips,),
        out_shape=[shape(plane.chips, width, part)] * 2,
        in_specs=[SMEM, whole_spec(left.shape), whole_spec(right.shape)],
        out_specs=[chip_spec(width, part)] * 2,
        scratch_shapes=[
            pltpu.VMEM((width, rows), bf16),
            pltpu.VMEM((plane.size, rows, part), bf16),
        ],
        name="out_weight_parts",
    )(plane.me.astype(jnp.int32)[None] % 2, left, right)


def columns_of(plane, pieces, layout):
    rows = pieces[0].shape[0]
    cols = pieces[0].shape[1]
    count = len(pieces)
    step = 80 if rows % 80 == 0 else rows
    widths = [sum(min(plane.size * n, most) for _, n, most in groups) for groups in layout]

    def kernel(places, *refs):
        parts, outs, scratch = refs[:count], refs[count:-1], refs[-1]
        for slot in range(count):
            scratch[places[slot]] = parts[slot][...]
        for out, groups in zip(outs, layout):
            base = 0
            for first, n, most in groups:
                for j in range(plane.size):
                    take = min(n, most - j * n)
                    if take > 0:
                        out[:, base + j * n : base + j * n + take] = scratch[
                            j, :, first : first + take
                        ].astype(f32)
                base += min(plane.size * n, most)

    return pl.pallas_call(
        kernel,
        grid=(rows // step,),
        out_shape=[shape(rows, w, dtype=f32) for w in widths],
        in_specs=[SMEM] + [rows_spec(step, cols)] * count,
        out_specs=[rows_spec(step, w) for w in widths],
        scratch_shapes=[pltpu.VMEM((count, step, cols), bf16)],
        name="columns_of",
    )(plane.places, *pieces)


def rows_of(plane, pieces):
    rows, cols = pieces[0].shape
    count = len(pieces)

    def kernel(places, *refs):
        parts, out, (buffer, sems) = refs[:count], refs[count], refs[count + 1 :]
        copies = []
        for slot in range(count):
            half = slot % 2
            if slot >= 2:
                copies[slot - 2].wait()
            buffer[half] = parts[slot][...].astype(f32)
            to = pl.ds(pl.multiple_of(places[slot] * rows, rows), rows)
            copies.append(pltpu.make_async_copy(buffer.at[half], out.at[to], sems.at[half]))
            copies[slot].start()
        for copy in copies[-2:]:
            copy.wait()

    return pl.pallas_call(
        kernel,
        out_shape=shape(count * rows, cols, dtype=f32),
        in_specs=[SMEM] + [VMEM] * count,
        out_specs=ANY,
        scratch_shapes=[pltpu.VMEM((2, rows, cols), f32), pltpu.SemaphoreType.DMA((2,))],
        name="rows_of",
    )(plane.places, *pieces)


def on_device(
    layer_in, out_cot, first_gain, first_bias, qkv_weight, qv_bias, out_weight, out_bias,
    second_gain, second_bias, fc_weight, fc_bias, proj_weight, proj_bias
):
    size = lax.axis_size("ctx")
    line = lax.axis_size("fsdp")
    plane = Plane(size)
    me = plane.me
    own_tokens, own_cot = layer_in[0], out_cot[0]
    rows, width = own_tokens.shape
    length = rows * size
    piece = width // line
    hidden = fc_weight.shape[1]
    part = hidden // size
    heads = -(-H // size)
    span = heads * HD
    spread = size * span
    out_part = width // size

    vectors = jnp.concatenate(
        [
            first_gain[None], first_bias[None], qv_bias, out_bias[None], second_gain[None],
            second_bias[None], proj_bias[None], fc_bias.reshape(-1, piece),
        ],
        axis=0,
    )
    count = vectors.shape[0]
    padded = jnp.pad(qkv_weight, ((0, 0), (0, spread - width)))
    packed = [
        lax.dynamic_slice_in_dim(padded, i * width + me * span, span, axis=1) for i in range(3)
    ]
    packed.append(lax.dynamic_slice_in_dim(out_weight, me * out_part, out_part, axis=1))
    packed.append(vectors.T)
    used = 3 * span + out_part + count
    first_cols = -(-used // 128) * 128
    packed.append(jnp.zeros((piece, first_cols - used), bf16))
    first_set = line_gather(jnp.concatenate(packed, axis=1), line)

    second_set = jnp.concatenate(
        [
            lax.dynamic_slice_in_dim(fc_weight, me * part, part, axis=1),
            lax.dynamic_slice_in_dim(proj_weight, me * part, part, axis=0).T,
        ],
        axis=1,
    )
    second_set = lax.all_gather(second_set, "fsdp", axis=0, tiled=True)

    both = plane.gather(jnp.concatenate([own_tokens, own_cot], axis=0))
    both = plane.collect([v.reshape(2, rows, width) for v in both])
    all_tokens = both[:, 0].reshape(length, width)
    all_cot = both[:, 1].reshape(length, width)

    vectors = first_set[:, 3 * span + out_part : used].T.astype(f32)
    gain_one, bias_one, bias_q, bias_v, bias_out, gain_two, bias_two, bias_proj = (
        vectors[i : i + 1] for i in range(8)
    )
    bias_fc = vectors[8:].reshape(-1, line, piece).transpose(1, 0, 2).reshape(1, hidden)
    bias_fc = lax.dynamic_slice_in_dim(bias_fc, me * part, part, axis=1)

    def heads_of(vector):
        vector = jnp.pad(vector, ((0, 0), (0, spread - width)))
        return lax.dynamic_slice_in_dim(vector, me * span, span, axis=1)

    out_cols = plane.collect(plane.gather(first_set[:, 3 * span : 3 * span + out_part]))

    normed_one, queries, keys, values = project(
        plane, all_tokens, first_set, gain_one, bias_one, heads_of(bias_q), heads_of(bias_v), span
    )
    pieces, attn_t, log_total = attend(heads, plane, queries, keys, values)
    pieces = plane.exchange(pieces)
    resid, normed_two, attn_out = branch_norm(
        plane, pieces, out_cols, own_tokens, bias_out, gain_two, bias_two
    )

    normed_two = plane.collect(plane.gather(normed_two)).reshape(length, width)
    activated, d_pre, grad_bias_fc, mine, theirs = feed_forward(
        plane, normed_two, all_cot, second_set, bias_fc
    )
    d_norm_two = plane.scatter(mine, theirs)
    grad_proj = matmul(all_cot, activated, 0, 0).astype(bf16).reshape(line, piece, part)
    grad_proj = line_scatter(grad_proj)
    grad_fc = matmul(normed_two, d_pre, 0, 0).astype(bf16).reshape(line, piece, part)
    grad_fc = line_scatter(grad_fc)
    mine, theirs = partial_rows(plane, activated, second_set, part, part, "mlp_out")
    mlp_out = plane.scatter(mine, theirs)
    layer_out = resid + bias_proj
    for term in mlp_out:
        layer_out = layer_out + term.astype(f32)
    layer_out = layer_out.astype(bf16)[None]

    d_resid, d_branch, grad_gain_two, grad_bias_two, pieces = branch_back(
        plane, d_norm_two, resid, own_cot, gain_two, out_cols, span
    )
    cots = plane.exchange(pieces)
    grads = attend_back(heads, plane, queries, keys, values, cots, attn_t, log_total)
    mine, theirs = partial_rows(plane, grads, first_set, 0, 3 * span, "d_norm_one")
    d_norm_one = plane.scatter(mine, theirs)
    total = d_norm_one[0]
    for term in d_norm_one[1:]:
        total = total + term.astype(f32)
    d_in, grad_gain_one, grad_bias_one = norm_back(total, own_tokens.astype(f32), gain_one)
    grad_in = (d_resid + d_in).astype(bf16)[None]

    mine, theirs = out_weight_parts(plane, attn_out, d_branch, out_part)
    grad_out = plane.scatter(mine, theirs)
    total = grad_out[0]
    for term in grad_out[1:]:
        total = total + term.astype(f32)
    grad_qkv = matmul(normed_one, grads, 0, 0)
    third_set = jnp.concatenate(
        [
            grad_qkv.astype(bf16),
            total.astype(bf16),
            jnp.zeros((width, first_cols - 3 * span - out_part), bf16),
        ],
        axis=1,
    )
    third_set = line_scatter(third_set.reshape(line, piece, first_cols))

    grad_proj = rows_of(plane, plane.gather(grad_proj.T))
    (grad_fc,) = columns_of(plane, plane.gather(grad_fc), [[(0, part, hidden)]])
    grad_qkv, grad_out = columns_of(
        plane,
        plane.gather(third_set),
        [[(i * span, span, width) for i in range(3)], [(3 * span, out_part, width)]],
    )

    def summed(value):
        return jnp.sum(value.astype(f32), axis=0, keepdims=True)

    vectors = jnp.concatenate(
        [
            grad_gain_one, grad_bias_one, summed(d_branch), grad_gain_two, grad_bias_two,
            summed(own_cot), summed(grads[:, :span]), summed(grads[:, 2 * span :]),
            grad_bias_fc,
        ],
        axis=1,
    )
    vectors = plane.collect(plane.gather(vectors))[:, 0]
    by_token = jnp.sum(vectors[:, : 6 * width], axis=0).reshape(6, line, piece)
    vectors = vectors[:, 6 * width :]
    bias_parts = jnp.stack(
        [vectors[:, i * span : (i + 1) * span].reshape(spread)[:width] for i in range(2)]
    ).reshape(2, line, piece)
    hidden_part = vectors[:, 2 * span :].reshape(line, hidden // line)
    parts = jnp.concatenate(
        [
            by_token.transpose(1, 0, 2).reshape(line, 6 * piece),
            bias_parts.transpose(1, 0, 2).reshape(line, 2 * piece),
            hidden_part,
        ],
        axis=1,
    )
    at = lax.axis_index("fsdp")
    final = lax.dynamic_index_in_dim(parts, at, 0, keepdims=False)
    for step in range(1, line):
        sent = lax.dynamic_index_in_dim(parts, (at + step) % line, 0, keepdims=False)
        final = final + lax.ppermute(sent, "fsdp", [(i, (i + step) % line) for i in range(line)])
    singles = [final[i * piece : (i + 1) * piece] for i in range(8)]
    return (
        layer_out,
        grad_in,
        singles[0],
        singles[1],
        grad_qkv,
        jnp.stack(singles[6:8]),
        grad_out,
        singles[2],
        singles[3],
        singles[4],
        grad_fc,
        final[8 * piece :],
        grad_proj,
        singles[5],
    )


def solution(mesh):
    by_width = P("fsdp")
    tokens = P("fsdp", "ctx", None)
    matrix = P("fsdp", None)
    across = P(None, "fsdp")
    params = (
        by_width, by_width, matrix, across, matrix, by_width, by_width, by_width, matrix, by_width,
        across, by_width,
    )
    return jax.shard_map(
        on_device,
        mesh=mesh,
        in_specs=(tokens, tokens) + params,
        out_specs=(tokens, tokens) + params,
        check_vma=False,
    )
```

time: 847 us -> 1350 us (1.59)
  Pallas kernels: 20.6 us -> 750 us
  waiting for transfers between devices: 346 us -> 251 us
  other arithmetic: 71 us -> 14.4 us
  starting transfers between devices: 189 us -> 141 us
  matrix products: 57.1 us -> 20.7 us
    pallas_call x2 -> x21, Pallas kernels: 20.6 us -> 750 us  [the longest x4 526 us: collect(): pl.pallas_call(kernel, out_shape=shape(count, *dims, dtype=pieces[0].dtyp...]
    ppermute x20 -> x3, waiting for transfers between devices: 97.7 us -> 0.62 us  [on_device(): lax.ppermute(sent, 'fsdp', [(i, (i + step) % line) for i in range(line)])]
    ppermute x5 -> x1, waiting for transfers between devices: 55.1 us -> 7.84 us  [line_gather(): relay = lax.ppermute(cross, 'fsdp', [(2, 3), (1, 0)])]
    ppermute x20 -> x3, starting transfers between devices: 54.5 us -> 12 us  [on_device(): lax.ppermute(sent, 'fsdp', [(i, (i + step) % line) for i in range(line)])]
    ppermute x5 -> x1, starting transfers between devices: 19.9 us -> 60.4 us  [line_gather(): up = lax.ppermute(value, 'fsdp', [(0, 1), (1, 2), (2, 3)])]
    concatenate x17 -> x3, local copies, waits for them, and re-layouts: 41.4 us -> 1.68 us  [the longest x1 1.24 us: on_device(): both = plane.gather(jnp.concatenate([own_tokens, own_cot], axis=0))]
    ppermute x1 -> x19, local copies, waits for them, and re-layouts: 4.23 us -> 43.7 us  [to_slot(): return lax.ppermute(value, 'ctx', self._pairs(slot, -1))]
    ppermute x5 -> x1, waiting for transfers between devices: 28.9 us -> 65.7 us  [line_gather(): cross = lax.ppermute(value, 'fsdp', [(0, 2), (1, 3), (2, 0), (3, 1)])]
  transfers between devices with their start and end apart: 106 -> 90, of which waited for: 43 -> 31; matrix products, arithmetic and copies ran while one was open for 26% -> 11% of each run, Pallas kernels for 1% -> 54%
where the time goes in v2:
time: 1350 us; the launch traced here: 1340 us
  Pallas kernels  750 us (56%)
  waiting for transfers between devices  251 us (19%)
  local copies, waits for them, and re-layouts  144 us (11%)
  starting transfers between devices  141 us (10%)
  matrix products  20.7 us (2%)
  between operations  15.4 us (1%)
  other arithmetic  14.4 us (1%)
    pallas_call x4, Pallas kernels, collect(): pl.pallas_call(kernel, out_shape=shape(count, *dims, dtype=pieces[0].dtyp...  526 us
    ppermute x21, waiting for transfers between devices, from_slot(): return lax.ppermute(value, 'ctx', self._pairs(slot, 1))  107 us
    pallas_call x1, Pallas kernels, line_gather(): pl.pallas_call(kernel, out_shape=shape(size * rows, value.shape[1]), in_s...  100 us
    ppermute x58, waiting for transfers between devices, to_slot(): return lax.ppermute(value, 'ctx', self._pairs(slot, -1))  67.2 us
    ppermute x1, waiting for transfers between devices, line_gather(): cross = lax.ppermute(value, 'fsdp', [(0, 2), (1, 3), (2, 0), (3, 1)])  65.7 us
    ppermute x1, starting transfers between devices, line_gather(): up = lax.ppermute(value, 'fsdp', [(0, 1), (1, 2), (2, 3)])  60.4 us
    ppermute x19, local copies, waits for them, and re-layouts, to_slot(): return lax.ppermute(value, 'ctx', self._pairs(slot, -1))  43.7 us
    ppermute x58, starting transfers between devices, to_slot(): return lax.ppermute(value, 'ctx', self._pairs(slot, -1))  33.8 us
  transfers between devices with their start and end apart: 90, of which 31 were waited for; matrix products, arithmetic and copies ran while one was open for 11% of the time, Pallas kernels for 54%

profile of v2, /device:TPU:0, one launch (start us, length us, event | category | flops | bytes accessed | tf_op | source)
XLA Modules:
  0.0 1336.5 jit_solution(17370714584348963970)
XLA Ops:
  24.6 65.7 %collective-permute-done.2.cross_ref = bf16[400,1024]{1,0:T(8,128)(2,1)} collective-permute-done((bf16[400,1024]{1,0:T(8,128)(2,1)S(1)}, bf16[400,1024]{1,0:T(8,128)(2,1)}, u32[]{:S(2)}, u32[]{:S(2)}) %collective-permute-start.2) | collective-permute-done | bytes 819232 | tf_op jit(solution)/shard_map/ppermute | solution.py:160
  92.4 60.4 %collective-permute-start = (bf16[400,1024]{1,0:T(8,128)(2,1)S(1)}, bf16[400,1024]{1,0:T(8,128)(2,1)}, u32[]{:S(2)}, u32[]{:S(2)}) collective-permute-start(bf16[400,1024]{1,0:T(8,128)(2,1)S(1)} %concatenate.23.own_ref), channel_id=1, source_target_pairs={{0,1},{1,2},{2,3},{4,5},{5,6},{6,7},{8,9},{9,10},{10,11},{12,13},{... | collective-permute-start | bytes 2457608 | tf_op jit(solution)/shard_map/ppermute | solution.py:158
  175.0 100.4 %line_collect.1.w_ref = bf16[1600,1024]{1,0:T(8,128)(2,1)} custom-call(s32[1]{0:T(128)} %bitcast.8.at_ref, bf16[400,1024]{1,0:T(8,128)(2,1)} %copy-done.11, bf16[400,1024]{1,0:T(8,128)(2,1)} %collective-permute-done.up_ref, bf16[400,1024]{1,0:T(8,128)(2,1)} %collective-permute-done.1.down_ref, bf16[400,1024]{1,0:T(8,128)(2,1)} %collective-permute-done.2.cross_ref, ...), custom_call_target="tpu_custom_call" | custom-call | tf_op jit(solution)/shard_map/line_collect/pallas_call | solution.py:186
  289.4 208.3 %collect.5 = bf16[8,2,128,1600]{3,2,1,0:T(8,128)(2,1)} custom-call(s32[8]{0:T(128)} %stack.53.places, bf16[2,128,1600]{2,1,0:T(8,128)(2,1)} %bitcast.81, bf16[2,128,1600]{2,1,0:T(8,128)(2,1)} %bitcast.84, bf16[2,128,1600]{2,1,0:T(8,128)(2,1)} %bitcast.85, bf16[2,128,1600]{2,1,0:T(8,128)(2,1)} %bitcast.86, bf16[2,128,1600]{2,1,0:T(8,128)(2,1)} %bitcast.87, ...), custom_call_target="tpu_custom_call" | custom-call | tf_op jit(solution)/shard_map/collect/pallas_call | solution.py:144
  514.7 9.4 attend.1
  550.5 200.4 %collect.4.w_ref = bf16[8,1600,200]{2,1,0:T(8,128)(2,1)} custom-call(s32[8]{0:T(128)} %stack.53.places, bf16[1600,200]{1,0:T(8,128)(2,1)} %copy-done.7, bf16[1600,200]{1,0:T(8,128)(2,1)} %copy.79.refs_1_, bf16[1600,200]{1,0:T(8,128)(2,1)} %copy.80.refs_2_, bf16[1600,200]{1,0:T(8,128)(2,1)} %copy.81.refs_3_, bf16[1600,200]{1,0:T(8,128)(2,1)} %copy.82.refs_4_, ...), custom_call_target="tpu_custom_call" | custom-call | tf_op jit(solution)/shard_map/collect/pallas_call | solution.py:144
  760.8 10.3 collective-permute-done.27.refs_3_
  782.0 105.1 %collect.6 = bf16[8,128,1600]{2,1,0:T(8,128)(2,1)} custom-call(s32[8]{0:T(128)} %stack.53.places, bf16[128,1600]{1,0:T(8,128)(2,1)} %get-tuple-element.84.refs_0_, bf16[128,1600]{1,0:T(8,128)(2,1)} %copy-done.21, bf16[128,1600]{1,0:T(8,128)(2,1)} %copy-done.20, bf16[128,1600]{1,0:T(8,128)(2,1)} %copy-done.19, bf16[128,1600]{1,0:T(8,128)(2,1)} %copy-done.22, ...), custom_call_target="tpu_custom_call" | custom-call | tf_op jit(solution)/shard_map/collect/pallas_call | solution.py:144
  887.2 18.4 %feed_forward.1 = (bf16[1024,800]{1,0:T(8,128)(2,1)}, bf16[1024,800]{1,0:T(8,128)(2,1)}, f32[1,800]{1,0:T(1,128)}, bf16[4,128,1600]{2,1,0:T(8,128)(2,1)}, bf16[4,128,1600]{2,1,0:T(8,128)(2,1)}) custom-call(s32[1]{0:T(128)S(6)} %select_n.171.core, bf16[1024,1600]{1,0:T(8,128)(2,1)} %bitcast.73, bf16[1024,1600]{1,0:T(8,128)(2,1)} %bitcast.76, ...), custom_call_target="tpu_custom_call" | custom-call | tf_op jit(solution)/shard_map/feed_forward/pallas_call | solution.py:394
  948.6 9.3 collective-permute-done.37.refs_1_
  957.9 9.6 collective-permute-done.38.refs_2_
  998.9 10.9 attend_back.1.left_ref
  1035.3 9.4 collective-permute-done.64
  1046.1 11.5 collective-permute-done.63
  1075.4 8.9 mlp_out.1
  1139.0 12.5 collect.7
  1153.7 11.4 collective-permute-start.60
  1171.6 14.3 %collective-permute-done.81 = bf16[800,400]{0,1:T(8,128)(2,1)} collective-permute-done((bf16[800,400]{0,1:T(8,128)(2,1)}, bf16[800,400]{0,1:T(8,128)(2,1)}, u32[]{:S(2)}, u32[]{:S(2)}) %collective-permute-start.81) | collective-permute-done | bytes 640032 | tf_op jit(solution)/shard_map/ppermute | solution.py:84
  1187.6 13.8 %collective-permute-done.80 = bf16[800,400]{0,1:T(8,128)(2,1)} collective-permute-done((bf16[800,400]{0,1:T(8,128)(2,1)}, bf16[800,400]{0,1:T(8,128)(2,1)}, u32[]{:S(2)}, u32[]{:S(2)}) %collective-permute-start.80) | collective-permute-done | bytes 640032 | tf_op jit(solution)/shard_map/ppermute | solution.py:84
  1203.6 13.1 collective-permute-done.74.refs_3_
  1216.7 13.2 collective-permute-done.73.refs_2_
  1238.5 14.2 %collective-permute-done.67.refs_3_ = bf16[400,1024]{1,0:T(8,128)(2,1)} collective-permute-done((bf16[400,1024]{1,0:T(8,128)(2,1)}, bf16[400,1024]{1,0:T(8,128)(2,1)}, u32[]{:S(2)}, u32[]{:S(2)}) %collective-permute-start.67) | collective-permute-done | bytes 819232 | tf_op jit(solution)/shard_map/ppermute | solution.py:84
  1252.7 16.9 %collective-permute-done.66.refs_2_ = bf16[400,1024]{1,0:T(8,128)(2,1)} collective-permute-done((bf16[400,1024]{1,0:T(8,128)(2,1)}, bf16[400,1024]{1,0:T(8,128)(2,1)}, u32[]{:S(2)}, u32[]{:S(2)}) %collective-permute-start.66) | collective-permute-done | bytes 819232 | tf_op jit(solution)/shard_map/ppermute | solution.py:84
  1298.7 12.7 copy.132
  (449 shorter events, 361.0 us)
Async XLA Ops:
  7.2 879.9 %all-gather.2.cloned.1.call-start = ((), (), s32[]{:S(2)}) async-start(), calls=%async_computation.3 | async-start | bytes 6656000 | tf_op jit(solution)/shard_map/all_gather | solution.py:620
  11.9 1088.4 %reduce-scatter.8.cloned.1.call-start = ((), (), s32[]{:S(2)}) async-start(), calls=%async_computation.6 | async-start | bytes 4096000 | tf_op jit(solution)/shard_map/reduce_scatter | solution.py:197
  14.3 75.9 %collective-permute-start.2 = (bf16[400,1024]{1,0:T(8,128)(2,1)S(1)}, bf16[400,1024]{1,0:T(8,128)(2,1)}, u32[]{:S(2)}, u32[]{:S(2)}) collective-permute-start(bf16[400,1024]{1,0:T(8,128)(2,1)S(1)} %concatenate.23.own_ref), channel_id=1, source_target_pairs={{0,2},{1,3},{2,0},{3,1},{4,6},{5,7},{6,4},{7,5},{8,10},{9,11},{10,... | collective-permute-start | bytes 2457608 | tf_op jit(solution)/shard_map/ppermute | solution.py:160
  18.4 73.9 %collective-permute-start.1 = (bf16[400,1024]{1,0:T(8,128)(2,1)S(1)}, bf16[400,1024]{1,0:T(8,128)(2,1)}, u32[]{:S(2)}, u32[]{:S(2)}) collective-permute-start(bf16[400,1024]{1,0:T(8,128)(2,1)S(1)} %concatenate.23.own_ref), channel_id=1, source_target_pairs={{1,0},{2,1},{3,2},{5,4},{6,5},{7,6},{9,8},{10,9},{11,10},{13,12},{... | collective-permute-start | bytes 2457608 | tf_op jit(solution)/shard_map/ppermute | solution.py:159
  21.6 131.2 %collective-permute-start.14 = (bf16[256,1600]{0,1:T(8,128)(2,1)}, bf16[256,1600]{0,1:T(8,128)(2,1)}, u32[]{:S(2)}, u32[]{:S(2)}) collective-permute-start(bf16[256,1600]{0,1:T(8,128)(2,1)} %copy.89), channel_id=1, source_target_pairs={{0,4},{4,0},{8,12},{12,8},{16,20},{20,16},{24,28},{28,24},{1,5},{5... | collective-permute-start | bytes 2457608 | tf_op jit(solution)/shard_map/ppermute | solution.py:87
  21.6 132.5 %collective-permute-start.13 = (bf16[256,1600]{0,1:T(8,128)(2,1)}, bf16[256,1600]{0,1:T(8,128)(2,1)}, u32[]{:S(2)}, u32[]{:S(2)}) collective-permute-start(bf16[256,1600]{0,1:T(8,128)(2,1)} %copy.89), channel_id=1, source_target_pairs={{0,24},{4,28},{8,16},{12,20},{16,8},{20,12},{24,0},{28,4},{1,25},{... | collective-permute-start | bytes 2457608 | tf_op jit(solution)/shard_map/ppermute | solution.py:84
  24.0 130.2 %collective-permute-start.12 = (bf16[256,1600]{0,1:T(8,128)(2,1)}, bf16[256,1600]{0,1:T(8,128)(2,1)}, u32[]{:S(2)}, u32[]{:S(2)}) collective-permute-start(bf16[256,1600]{0,1:T(8,128)(2,1)} %copy.89), channel_id=1, source_target_pairs={{0,16},{4,20},{8,24},{12,28},{16,0},{20,4},{24,8},{28,12},{1,17},{... | collective-permute-start | bytes 2457608 | tf_op jit(solution)/shard_map/ppermute | solution.py:84
  92.4 74.8 %collective-permute-start = (bf16[400,1024]{1,0:T(8,128)(2,1)S(1)}, bf16[400,1024]{1,0:T(8,128)(2,1)}, u32[]{:S(2)}, u32[]{:S(2)}) collective-permute-start(bf16[400,1024]{1,0:T(8,128)(2,1)S(1)} %concatenate.23.own_ref), channel_id=1, source_target_pairs={{0,1},{1,2},{2,3},{4,5},{5,6},{6,7},{8,9},{9,10},{10,11},{12,13},{... | collective-permute-start | bytes 2457608 | tf_op jit(solution)/shard_map/ppermute | solution.py:158
  154.1 127.4 %collective-permute-start.17 = (bf16[256,1600]{0,1:T(8,128)(2,1)}, bf16[256,1600]{0,1:T(8,128)(2,1)}, u32[]{:S(2)}, u32[]{:S(2)}) collective-permute-start(bf16[256,1600]{0,1:T(8,128)(2,1)} %collective-permute-done.13), channel_id=1, source_target_pairs={{0,4},{4,0},{8,12},{12,8},{16,20},{20,16},{24,28},{28,24},{1,5},{5... | collective-permute-start | bytes 2457608 | tf_op jit(solution)/shard_map/ppermute | solution.py:87
  154.2 130.3 %collective-permute-start.16 = (bf16[256,1600]{0,1:T(8,128)(2,1)}, bf16[256,1600]{0,1:T(8,128)(2,1)}, u32[]{:S(2)}, u32[]{:S(2)}) collective-permute-start(bf16[256,1600]{0,1:T(8,128)(2,1)} %collective-permute-done.12), channel_id=1, source_target_pairs={{0,4},{4,0},{8,12},{12,8},{16,20},{20,16},{24,28},{28,24},{1,5},{5... | collective-permute-start | bytes 2457608 | tf_op jit(solution)/shard_map/ppermute | solution.py:87
  154.7 132.5 %collective-permute-start.15 = (bf16[256,1600]{0,1:T(8,128)(2,1)}, bf16[256,1600]{0,1:T(8,128)(2,1)}, u32[]{:S(2)}, u32[]{:S(2)}) collective-permute-start(bf16[256,1600]{0,1:T(8,128)(2,1)} %collective-permute-done.11), channel_id=1, source_target_pairs={{0,4},{4,0},{8,12},{12,8},{16,20},{20,16},{24,28},{28,24},{1,5},{5... | collective-permute-start | bytes 2457608 | tf_op jit(solution)/shard_map/ppermute | solution.py:87
  279.0 256.5 %collective-permute-start.7 = (bf16[1600,200]{0,1:T(8,128)(2,1)}, bf16[1600,200]{0,1:T(8,128)(2,1)S(1)}, u32[]{:S(2)}, u32[]{:S(2)}) collective-permute-start(bf16[1600,200]{0,1:T(8,128)(2,1)} %copy.75), channel_id=1, source_target_pairs={{0,4},{4,0},{8,12},{12,8},{16,20},{20,16},{24,28},{28,24},{1,5},{5... | collective-permute-start | bytes 1920008 | tf_op jit(solution)/shard_map/ppermute | solution.py:87
  279.0 220.0 %collective-permute-start.6 = (bf16[1600,200]{0,1:T(8,128)(2,1)}, bf16[1600,200]{0,1:T(8,128)(2,1)S(1)}, u32[]{:S(2)}, u32[]{:S(2)}) collective-permute-start(bf16[1600,200]{0,1:T(8,128)(2,1)} %copy.75), channel_id=1, source_target_pairs={{0,24},{4,28},{8,16},{12,20},{16,8},{20,12},{24,0},{28,4},{1,25},{... | collective-permute-start | bytes 1920008 | tf_op jit(solution)/shard_map/ppermute | solution.py:84
  281.5 217.4 %collective-permute-start.5 = (bf16[1600,200]{0,1:T(8,128)(2,1)}, bf16[1600,200]{0,1:T(8,128)(2,1)S(1)}, u32[]{:S(2)}, u32[]{:S(2)}) collective-permute-start(bf16[1600,200]{0,1:T(8,128)(2,1)} %copy.75), channel_id=1, source_target_pairs={{0,16},{4,20},{8,24},{12,28},{16,0},{20,4},{24,8},{28,12},{1,17},{... | collective-permute-start | bytes 1920008 | tf_op jit(solution)/shard_map/ppermute | solution.py:84
  284.5 215.0 %collective-permute-start.4 = (bf16[1600,200]{0,1:T(8,128)(2,1)}, bf16[1600,200]{0,1:T(8,128)(2,1)}, u32[]{:S(2)}, u32[]{:S(2)}) collective-permute-start(bf16[1600,200]{0,1:T(8,128)(2,1)} %copy.75), channel_id=1, source_target_pairs={{0,8},{4,12},{8,0},{12,4},{16,24},{20,28},{24,16},{28,20},{1,9},{5... | collective-permute-start | bytes 1920008 | tf_op jit(solution)/shard_map/ppermute | solution.py:84
  533.2 217.7 %collective-permute-start.20 = (bf16[128,256]{1,0:T(8,128)(2,1)}, bf16[128,256]{1,0:T(8,128)(2,1)S(1)}, u32[]{:S(2)}, u32[]{:S(2)}) collective-permute-start(bf16[128,256]{1,0:T(8,128)(2,1)} %get-tuple-element.78), channel_id=1, source_target_pairs={{0,24},{4,28},{8,16},{12,20},{16,8},{20,12},{24,0},{28,4},{1,25},{... | collective-permute-start | bytes 196616 | tf_op jit(solution)/shard_map/ppermute | solution.py:87
  535.5 215.4 %collective-permute-start.21 = (bf16[128,256]{1,0:T(8,128)(2,1)}, bf16[128,256]{1,0:T(8,128)(2,1)S(1)}, u32[]{:S(2)}, u32[]{:S(2)}) collective-permute-start(bf16[128,256]{1,0:T(8,128)(2,1)} %get-tuple-element.79), channel_id=1, source_target_pairs={{0,4},{4,0},{8,12},{12,8},{16,20},{20,16},{24,28},{28,24},{1,5},{5... | collective-permute-start | bytes 196616 | tf_op jit(solution)/shard_map/ppermute | solution.py:87
  535.5 215.4 %collective-permute-start.22 = (bf16[128,256]{1,0:T(8,128)(2,1)}, bf16[128,256]{1,0:T(8,128)(2,1)S(1)}, u32[]{:S(2)}, u32[]{:S(2)}) collective-permute-start(bf16[128,256]{1,0:T(8,128)(2,1)} %get-tuple-element.80), channel_id=1, source_target_pairs={{0,12},{4,8},{8,4},{12,0},{16,28},{20,24},{24,20},{28,16},{1,13},{... | collective-permute-start | bytes 196616 | tf_op jit(solution)/shard_map/ppermute | solution.py:87
  536.3 214.6 %collective-permute-start.23 = (bf16[128,256]{1,0:T(8,128)(2,1)}, bf16[128,256]{1,0:T(8,128)(2,1)S(1)}, u32[]{:S(2)}, u32[]{:S(2)}) collective-permute-start(bf16[128,256]{1,0:T(8,128)(2,1)} %get-tuple-element.81), channel_id=1, source_target_pairs={{0,20},{4,16},{8,28},{12,24},{16,4},{20,0},{24,12},{28,8},{1,21},{... | collective-permute-start | bytes 196616 | tf_op jit(solution)/shard_map/ppermute | solution.py:87
  536.5 214.5 %collective-permute-start.24 = (bf16[128,256]{1,0:T(8,128)(2,1)}, bf16[128,256]{1,0:T(8,128)(2,1)S(1)}, u32[]{:S(2)}, u32[]{:S(2)}) collective-permute-start(bf16[128,256]{1,0:T(8,128)(2,1)} %get-tuple-element.82), channel_id=1, source_target_pairs={{0,28},{4,24},{8,20},{12,16},{16,12},{20,8},{24,4},{28,0},{1,29},{... | collective-permute-start | bytes 196616 | tf_op jit(solution)/shard_map/ppermute | solution.py:87
  922.7 247.1 %reduce-scatter.6.cloned.1.call-start = ((), (), s32[]{:S(2)}) async-start(), calls=%async_computation.5 | async-start | bytes 3584000 | tf_op jit(solution)/shard_map/reduce_scatter | solution.py:197
  939.0 291.4 %reduce-scatter.4.cloned.1.call-start = ((), (), s32[]{:S(2)}) async-start(), calls=%async_computation.4 | async-start | bytes 4096000 | tf_op jit(solution)/shard_map/reduce_scatter | solution.py:197
  1238.0 73.4 %collective-permute-start.76 = (bf16[400,800]{1,0:T(8,128)(2,1)}, bf16[400,800]{1,0:T(8,128)(2,1)}, u32[]{:S(2)}, u32[]{:S(2)}) collective-permute-start(bf16[400,800]{1,0:T(8,128)(2,1)} %collective-permute-done.72.refs_1_), channel_id=1, source_target_pairs={{0,4},{4,0},{8,12},{12,8},{16,20},{20,16},{24,28},{28,24},{1,5},{5... | collective-permute-start | bytes 1920008 | tf_op jit(solution)/shard_map/ppermute | solution.py:87
  1238.0 81.9 %collective-permute-start.68 = (bf16[400,1024]{1,0:T(8,128)(2,1)}, bf16[400,1024]{1,0:T(8,128)(2,1)S(1)}, u32[]{:S(2)}, u32[]{:S(2)}) collective-permute-start(bf16[400,1024]{1,0:T(8,128)(2,1)} %bitcast.99), channel_id=1, source_target_pairs={{0,4},{4,0},{8,12},{12,8},{16,20},{20,16},{24,28},{28,24},{1,5},{5... | collective-permute-start | bytes 2457608 | tf_op jit(solution)/shard_map/ppermute | solution.py:87
  (140 other events, 2750.1 us)
Sparse Core Ops, SparseCore 0:
  12.0 145.7 all-gather.1
  922.8 69.5 reduce-scatter.7
  995.3 56.2 reduce-scatter.5
  1065.3 69.6 reduce-scatter.3
